TPU v7x, 256 devices: a whole 4x4x8 slice. The times are simulated.
256 devices in a mesh: prow: 2 (over core), pcol: 128 (over z, y, x).
Axes of the slice: x: 4, y: 4, z: 8, core: 2. Of those that a mesh axis runs over, the one named last changes fastest.
Arguments:
- matrix: float32 [8192, 49152], P('prow', 'pcol'), may hold values from -8 to 8, as said below
- pivot_rows: int32 [128], replicated, may hold values from 0 to 8191, as said below
Outputs:
- factored: float32 [8192, 49152], P('prow', 'pcol')
Inputs may be any that keep to these rules, and one draw needn't show every extreme that they name: `pivot_rows`: 128 distinct row indices; exactly 32 of them are below 128. `matrix`: in row pivot_rows[k] the entry of column k has magnitude 4 or more and the other entries of the first 128 columns have magnitude 0.3 or less; the LU factorization without row exchanges of the pivot block has all its diagonal entries of magnitude 1 or more.
All inputs are finite; a program needn't handle non-finite values.
Results may differ from a plain program's by a relative error of at most 0.0003.
Values may be sent and summed in bfloat16 or wider, within the bound.
A program may use at most 128 MiB of HBM per device.

v0:
```python
import jax
import jax.numpy as jnp
from jax import lax
from jax.sharding import PartitionSpec as P

NB = 128


HIGH = lax.Precision.HIGHEST


def copy_for_each(value, axis):
    copies = jnp.broadcast_to(value, (lax.axis_size(axis), *value.shape))
    return lax.all_to_all(copies, axis, split_axis=0, concat_axis=0, tiled=True)


def of_everyone(value, axis):
    everything = copy_for_each(value, axis)
    return jnp.sum(everything, axis=0)


def broadcast(value, axis, root):
    mine = lax.axis_index(axis) == root
    return lax.psum(jnp.where(mine, value, jnp.zeros_like(value)), axis)


def matmul(left, right):
    return jnp.dot(left, right, precision=HIGH, preferred_element_type=jnp.float32)


def nilpotent_inverse(strict):
    length = strict.shape[0]
    result = jnp.eye(length, dtype=jnp.float32) + strict
    power = strict
    reach = 2
    while reach < length:
        power = matmul(power, power)
        result = result + matmul(result, power)
        reach = reach * 2
    return result


def unit_lower_inverse(low):
    return nilpotent_inverse(-jnp.tril(low, -1))


def upper_inverse(upp):
    diag_vals = jnp.diagonal(upp)
    scaled = jnp.triu(upp, 1) / diag_vals[:, None]
    return nilpotent_inverse(-scaled) / diag_vals[None, :]


def small_factor(block):
    length = block.shape[0]
    for column in range(length - 1):
        factor_col = block[column + 1 :, column] / block[column, column]
        block = block.at[column + 1 :, column].set(factor_col)
        block = block.at[column + 1 :, column + 1 :].add(
            -factor_col[:, None] * block[column, column + 1 :][None, :]
        )
    return block


def factor(block):
    length = block.shape[0]
    if length <= 16:
        return small_factor(block)
    middle = length // 2
    top = factor(block[:middle, :middle])
    right_part = matmul(unit_lower_inverse(top), block[:middle, middle:])
    down_part = matmul(block[middle:, :middle], upper_inverse(jnp.triu(top)))
    schur = block[middle:, middle:] - matmul(down_part, right_part)
    bottom = factor(schur)
    return jnp.concatenate(
        [jnp.concatenate([top, right_part], 1), jnp.concatenate([down_part, bottom], 1)], 0
    )


def rank_order(values):
    count = values.shape[0]
    ladder = jnp.arange(count, dtype=jnp.int32)
    before = (values[None, :] < values[:, None]) | (values[None, :] == values[:, None]) & (
        ladder[None, :] < ladder[:, None]
    )
    ranks = jnp.sum(before.astype(jnp.int32), axis=1)
    placed = (ranks[:, None] == ladder[None, :]).astype(jnp.int32)
    return jnp.sum(placed * values[:, None], axis=0)


def swap_lists(pivot_rows):
    ladder = jnp.arange(NB, dtype=jnp.int32)
    sentinel = jnp.int32(2**30)
    chosen = jnp.any(pivot_rows[:, None] == ladder[None, :], axis=0)
    displaced = rank_order(jnp.where(chosen, sentinel, ladder))
    landing = rank_order(jnp.where(pivot_rows >= NB, pivot_rows, sentinel))
    return (landing, displaced)


def split_three(source):
    first = source.astype(jnp.bfloat16)
    rest = source - lax.optimization_barrier(first).astype(jnp.float32)
    second = rest.astype(jnp.bfloat16)
    third = (rest - lax.optimization_barrier(second).astype(jnp.float32)).astype(jnp.bfloat16)
    return jnp.stack([first, second, third])


def fetch_rows(matrix, wanted, row_start):
    local = wanted - row_start
    inside = (local >= 0) & (local < matrix.shape[0])
    picked = matrix[jnp.clip(local, 0, matrix.shape[0] - 1)]
    return jnp.where(inside[:, None], picked, 0.0)


def panel_factors(pivot_block, panel_rows, below):
    packed = factor(pivot_block)
    diag_lower = jnp.tril(packed, -1) + jnp.eye(NB, dtype=jnp.float32)
    lower = matmul(panel_rows, upper_inverse(jnp.triu(packed)))
    lower = jnp.where(below[:, None], lower, 0.0)
    return (packed, diag_lower, lower)


def on_device(matrix, pivot_rows):
    rows_dev, cols_dev = matrix.shape
    row_start = lax.axis_index("prow") * rows_dev
    col_index = lax.axis_index("pcol")
    landing, displaced = swap_lists(pivot_rows)
    wanted = jnp.concatenate([pivot_rows, displaced])
    moved = of_everyone(fetch_rows(matrix, wanted, row_start), "prow")
    incoming = moved[:NB]
    returning = moved[NB:]
    targets = jnp.concatenate([jnp.arange(NB, dtype=jnp.int32), landing]) - row_start
    inside = (targets >= 0) & (targets < rows_dev)
    safe_targets = jnp.where(inside, targets, rows_dev)
    swapped = matrix.at[safe_targets].set(jnp.concatenate([incoming, returning], 0), mode="drop")
    below = row_start + jnp.arange(rows_dev, dtype=jnp.int32) >= NB
    panel_rows, pivot_block = (
        broadcast(swapped[:, :NB], "pcol", 0),
        broadcast(incoming[:, :NB], "pcol", 0),
    )
    packed, diag_lower, lower = panel_factors(pivot_block, panel_rows, below)
    lower_slices = split_three(lower)
    upper = matmul(unit_lower_inverse(diag_lower), incoming)
    upper_slices = split_three(upper)
    left_order = (0, 0, 0, 1, 1, 1, 2, 2, 2)
    right_order = (0, 1, 2, 0, 1, 2, 0, 1, 2)
    left_stack = jnp.concatenate([lower_slices[i] for i in left_order], axis=1)
    right_stack = jnp.concatenate([upper_slices[j] for j in right_order], axis=0)
    update = jnp.dot(left_stack, right_stack, preferred_element_type=jnp.float32)
    result = swapped - update
    result = result.at[:NB].set(jnp.where(row_start == 0, upper, result[:NB]))
    panel_out = lower.at[:NB].set(jnp.where(row_start == 0, packed, lower[:NB]))
    result = result.at[:, :NB].set(jnp.where(col_index == 0, panel_out, result[:, :NB]))
    return result


def solution(mesh):
    in_specs = (P("prow", "pcol"), P())
    out_specs = P("prow", "pcol")
    return jax.shard_map(
        on_device, mesh=mesh, in_specs=in_specs, out_specs=out_specs, check_vma=False
    )
```

profile of v0, /device:TPU:2, one launch (start us, length us, event | category | flops | bytes accessed | tf_op | source)
XLA Modules:
  0.0 612.5 jit_solution(1971046099091969851)
XLA Ops:
  6.5 5.9 copy.270
  12.9 3.9 gather_fusion
  16.9 0.9 broadcast_in_dim.92
  17.9 3.5 all-to-all-start
  21.8 1.5 all-to-all-done
  23.4 7.0 %scatter_fusion = f32[4096,384]{1,0:T(8,128)} fusion(f32[4096,384]{1,0:T(8,128)} %copy.270, s32[256]{0:T(256)S(1)} %bitcast.585, f32[256,384]{1,0:T(8,128)S(1)} %reduce_sum.49), kind=kCustom, calls=%fused_computation.9 | custom fusion | bytes 1180672 | tf_op jit(solution)/shard_map/scatter | solution.py:134
  31.1 3.0 slice_select_fusion
  34.9 231.4 %all-reduce.3.cloned.1.call-done = (f32[4096,128]{1,0:T(8,128)}, f32[128,128]{1,0:T(8,128)}) async-done(((f32[4096,128]{1,0:T(8,128)}, f32[128,128]{1,0:T(8,128)}), (f32[4096,128]{1,0:T(8,128)}, f32[128,128]{1,0:T(8,128)})) %all-reduce.3.cloned.1.call-update) | async-done | bytes 2162704 | tf_op jit(solution)/shard_map/psum | solution.py:24
  266.3 0.8 slice.6835
  267.1 1.2 slice.6837
  268.3 1.4 negate_reduce_fusion.55
  305.6 0.8 fusion.64
  306.8 0.9 fusion.66
  307.7 0.8 convolution_subtract_fusion.7
  346.3 0.9 fusion.40
  348.0 0.9 fusion.42
  348.9 0.9 convolution_subtract_fusion.3
  422.6 0.8 gather_fusion.4
  447.2 0.7 negate_reduce_fusion.70
  449.3 0.7 negate_reduce_fusion.69
  451.4 0.7 negate_reduce_fusion.68
  453.5 0.7 negate_reduce_fusion.95
  455.6 0.7 negate_reduce_fusion.94
  457.7 0.7 negate_reduce_fusion.107
  486.3 0.7 negate_reduce_fusion.66
  494.7 0.7 negate_reduce_fusion.92
  496.8 0.7 negate_reduce_fusion.106
  581.4 1.2 gather_fusion.8
  586.1 2.0 constant_dynamic-update-slice_fusion.8
  593.2 5.4 convolution_subtract_fusion
  598.7 2.7 copy-done.1
  601.4 3.8 fusion
  (907 shorter events, 287.9 us)
Async XLA Ops:
  6.5 5.9 copy-start.3
  17.9 5.5 all-to-all-start
  21.4 244.9 %all-reduce.3.cloned.1.call-start = ((), (), s32[]{:S(2)}) async-start(), calls=%async_computation.1 | async-start | bytes 4325376 | tf_op jit(solution)/shard_map/psum | solution.py:24
  266.3 159.6 %copy-start.2 = (f32[128,128]{1,0:T(8,128)S(1)}, f32[128,128]{1,0:T(8,128)}, u32[]{:S(2)}) copy-start(f32[128,128]{1,0:T(8,128)} %get-tuple-element.2922) | copy-start | bytes 196612
  425.7 160.4 %copy-start = (f32[4096,128]{1,0:T(8,128)S(1)}, f32[4096,128]{1,0:T(8,128)}, u32[]{:S(2)}) copy-start(f32[4096,128]{1,0:T(8,128)} %get-tuple-element.2921) | copy-start | bytes 6291460
  589.7 3.6 slice-start
  590.2 3.0 slice-start.1
  598.7 2.7 copy-start.1
Sparse Core Ops, SparseCore 0:
  34.2 232.0 all-reduce.2
where the time goes:
time: 617 us; the launch traced here: 612 us
  waiting for transfers between devices  233 us (38%)
  local copies, waits for them, and re-layouts  204 us (33%)
  other arithmetic  98.5 us (16%)
  matrix products  37 us (6%)
  between operations  36.2 us (6%)
    psum x1, waiting for transfers between devices, broadcast(): return lax.psum(jnp.where(mine, value, jnp.zeros_like(value)), axis)  231 us
    neg x112, other arithmetic, small_factor(): -factor_col[:, None] * block[column, column + 1:][None, :]  79.3 us
    scatter-add x120, local copies, waits for them, and re-layouts, small_factor(): block.at[column + 1:, column + 1:]  64.1 us
    slice x120, local copies, waits for them, and re-layouts, small_factor(): factor_col = block[column + 1:, column] / block[column, column]  63.1 us
    scatter x120, local copies, waits for them, and re-layouts, small_factor(): block = block.at[column + 1:, column].set(factor_col)  34.8 us
    dot_general x147, matrix products, matmul(): jnp.dot(left, right, precision=HIGH, preferred_element_type=jnp.float32)  31.6 us
  transfers between devices with their start and end apart: 2, of which 2 were waited for; matrix products, arithmetic and copies ran while one was open for 0% of the time, Pallas kernels for 0%

commit v1 on v0

v1 whole, which is shorter than its diff:
```python
import functools

import jax
import jax.numpy as jnp
from jax import lax
from jax.experimental import pallas as pl
from jax.experimental.pallas import tpu as pltpu
from jax.sharding import PartitionSpec as P

NB = 128
FEW = 96
F32 = jnp.float32
BF16 = jnp.bfloat16
I32 = jnp.int32
HIGH = lax.Precision.HIGHEST
MESH = pl.DeviceIdType.MESH

TREES_A = (
    4196353, 201523325, 268626057, 201455808, 124977344, 180617363, 230918337, 144870656,
    174326016, 239403250, 289687809, 205753664, 201523392, 268697770, 335759561, 268592384,
    201523392, 268697755, 335763673, 268588288, 166985984, 226820307, 277104897, 209917248,
    208994624, 289800451, 356845905, 272893312, 268697856, 335872194, 402917649, 335742272,
    268697856, 335872218, 402942229, 335770944, 233111872, 278266134, 361056577, 293868928,
    291897728, 340197714, 407243137, 340069824, 335872320, 403046658, 470108481, 402916736,
    335872320, 403046682, 470108493, 402945408, 295043456, 348586306, 411457941, 344282560,
    359072192, 408420754, 474417617, 407242240, 403046784, 470221122, 537282961, 470107584,
    403046784, 478609735, 545655169, 604308928, 344392128, 412615042, 482806209, 545654272,
    409469440, 470352322, 537397761, 482807360, 470221248, 537395586, 604441025, 537273856,
    335872320, 403046671, 470092097, 402926976, 279314816, 383189315, 411441537, 344266176,
    340197824, 440926594, 474417601, 409339392, 403046784, 470221155, 537266561, 470093248,
    268697856, 335872231, 402917653, 335789392, 247791936, 311820546, 344295749, 281320832,
    307626368, 341246306, 407243169, 373624256, 335872320, 403046658, 470092097, 402918784,
    201523392, 268697766, 335751488, 268608896, 178520320, 244646083, 277088513, 247661888,
    205848896, 274071843, 340068673, 272895360, 268697856, 335872227, 402917665, 335742272,
)
TREES_B = (
    33570824, 201523392, 268697856, 201523392, 201523392, 268697856, 335872320, 268697856,
    268697770, 335872200, 403046664, 335872202, 201523323, 268697788, 335872228, 268697766,
    469859520, 538083584, 604217664, 537049344, 537036032, 604210496, 671388032, 604209472,
    604210394, 671383832, 738558280, 671400200, 537044126, 604225741, 671400204, 604217540,
    436370688, 503517504, 537137536, 503515456, 503519552, 570708352, 637862336, 570687872,
    570687752, 637862217, 705036696, 637878600, 503515351, 570687765, 637870404, 570687756,
    369327424, 436479360, 503656896, 436470144, 436476288, 503648704, 570819072, 503644608,
    503644488, 570835336, 637993416, 570835336, 436488478, 503660893, 570827140, 503644492,
    306470272, 373637568, 440812160, 373639616, 369446336, 436617728, 503792200, 436619776,
    438714760, 503792072, 570966540, 503794120, 370501964, 446054796, 512180800, 436619660,
    250954048, 303448448, 369574336, 310788480, 275136896, 336019904, 403194368, 338117056,
    372719946, 404242825, 470368744, 403194248, 302399759, 336019789, 403194244, 371671396,
    183910656, 210190656, 268976512, 203882816, 208093504, 307773824, 336150976, 268976512,
    271073546, 336150856, 403325320, 336150856, 203899110, 303579405, 344539468, 268976388,
    116850880, 152568064, 218694976, 164233472, 152568064, 256442688, 290062720, 220791104,
    218693864, 285868296, 353042760, 285868296, 160956580, 219742444, 285868300, 227082444,
)
DEEPEST = 11

TREES = 6
CHUNKS = 8
PIECE = 88
SPAN = PIECE * CHUNKS
TAIL = 48
EXT = 4096
INV = TREES * SPAN
HELD = INV + TREES * TAIL


def swap_lists(pivot_col, pivot_row, row_start, tab_ref):
    lane = lax.broadcasted_iota(I32, (NB, NB), 1)
    sub = lax.broadcasted_iota(I32, (NB, NB), 0)
    low = pivot_col >= NB
    smaller = (pivot_row < pivot_col) & (pivot_row >= NB)
    rank = jnp.sum(jnp.where(smaller, 1.0, 0.0), axis=1, keepdims=True)
    lane_f = lane.astype(F32)
    hit = (rank == lane_f) & low
    landing = jnp.sum(jnp.where(hit, pivot_col.astype(F32), 0.0), axis=0, keepdims=True)
    chosen = jnp.sum(jnp.where(pivot_col == lane, 1.0, 0.0), axis=0, keepdims=True)
    free = jnp.broadcast_to(1.0 - chosen, (NB, NB))
    ahead = jnp.sum(jnp.where(lane < sub, free, 0.0), axis=1, keepdims=True)
    own = jnp.sum(jnp.where(lane == sub, free, 0.0), axis=1, keepdims=True)
    place = (ahead == lane_f) & (own > 0.5)
    displaced = jnp.sum(jnp.where(place, sub.astype(F32), 0.0), axis=0, keepdims=True)
    bound = row_start + lane * TILE
    starts = jnp.sum(jnp.where(low & (pivot_col < bound), 1.0, 0.0), axis=0, keepdims=True)
    tab_ref[...] = jnp.concatenate(
        [landing, displaced, starts, jnp.zeros((5, NB), F32)], axis=0
    ).astype(I32)


def gather_kernel(pivots_sm, pivots_v, matrix, rows_ref, mask_ref, tab_ref, tab_sm, sems):
    rows_dev = matrix.shape[0]
    row_start = lax.axis_index("prow") * rows_dev

    def fetch(source, k):
        local = jnp.clip(source - row_start, 0, rows_dev - 1)
        pltpu.make_async_copy(
            matrix.at[pl.ds(local, 1), :], rows_ref.at[pl.ds(k, 1), :], sems.at[0]
        ).start()

    def first(i, carry):
        for j in range(8):
            k = 8 * i + j
            fetch(pivots_sm[k], k)
        return carry

    lax.fori_loop(0, NB // 8, first, 0)
    pivot_row = jnp.broadcast_to(pivots_v[...], (NB, NB))
    pivot_col = jnp.transpose(pivot_row.astype(F32)).astype(I32)
    swap_lists(pivot_col, pivot_row, row_start, tab_ref)
    move = pltpu.make_async_copy(tab_ref, tab_sm, sems.at[1])
    move.start()
    inside = (pivot_col >= row_start) & (pivot_col < row_start + rows_dev)
    mask_ref[...] = jnp.where(inside, 1.0, 0.0)
    move.wait()

    def second(i, carry):
        for j in range(8):
            k = 8 * i + j
            fetch(tab_sm[1, k], NB + k)
        return carry

    lax.fori_loop(0, FEW // 8, second, 0)
    pltpu.make_async_copy(
        matrix.at[pl.ds(0, NB + FEW), :], rows_ref, sems.at[0]
    ).wait()


def gather(matrix, pivot_rows):
    cols = matrix.shape[1]
    return pl.pallas_call(
        gather_kernel,
        name="gather_rows",
        out_shape=(
            jax.ShapeDtypeStruct((NB + FEW, cols), F32),
            jax.ShapeDtypeStruct((NB, NB), F32),
            jax.ShapeDtypeStruct((8, NB), I32),
        ),
        in_specs=[
            pl.BlockSpec(memory_space=pltpu.SMEM),
            pl.BlockSpec(memory_space=pltpu.VMEM),
            pl.BlockSpec(memory_space=pl.ANY),
        ],
        out_specs=(pl.BlockSpec(memory_space=pltpu.VMEM),) * 3,
        scratch_shapes=[pltpu.SMEM((8, NB), I32), pltpu.SemaphoreType.DMA((2,))],
    )(pivot_rows, pivot_rows.reshape(1, NB), matrix)


def pick(values, bits):
    while len(values) > 1:
        bit, bits = bits[0], bits[1:]
        values = [
            lo if isinstance(lo, int) and lo == hi else jnp.where(bit, hi, lo)
            for lo, hi in zip(values[::2], values[1::2])
        ]
    return values[0]


def eliminate(block, packed_ref, linv_ref, binv_ref, upper_ref, scale_ref):
    lane = lax.broadcasted_iota(I32, (8, NB), 1)
    sub = lax.broadcasted_iota(I32, (8, NB), 0)
    groups = NB // 8
    left = tuple(block[8 * q : 8 * q + 8, :] for q in range(groups))
    right = tuple(jnp.where(lane == sub + 8 * q, 1.0, 0.0) for q in range(groups))

    def row_of(x, k):
        return jnp.broadcast_to(x[k : k + 1, :], (8, NB))

    def column_of(x, k):
        return jnp.broadcast_to(x[:, k : k + 1], (8, NB))

    def turn(g, carry):
        a, z = list(carry[0]), list(carry[1])
        active = lane < NB - 8 * g
        upper, linv, scale = a[0], z[0], jnp.zeros((8, NB), F32)
        column = [column_of(a[0], j) for j in range(8)]
        for k in range(8):
            pivot = row_of(column[k], k)
            row_a, row_z = row_of(a[0], k), row_of(z[0], k)
            inverse = 1.0 / pivot
            here = sub == k
            upper = jnp.where(here, row_a, upper)
            linv = jnp.where(here, row_z, linv)
            scale = jnp.where(here, inverse, scale)
            row_a = jnp.where(
                lane > k, jnp.where(active, row_a, 0.0), jnp.where(lane == k, pivot - 1.0, 0.0)
            )
            first = jnp.where(here, 0.0, column[k] * inverse)
            for j in range(k + 1, 8):
                column[j] = column[j] - first * row_of(column[j], k)
            for q in range(groups):
                factor = first if q == 0 else column_of(a[q], k) * inverse
                a[q] = a[q] - factor * row_a
                z[q] = z[q] - factor * row_z
        at = pl.ds(pl.multiple_of(8 * g, 8), 8)
        upper_ref[at, :] = upper
        linv_ref[at, :] = linv
        scale_ref[at, :] = scale
        a = [pltpu.roll(x, NB - 8, 1) for x in a]
        return tuple(a[1:] + a[:1]), tuple(z[1:] + z[:1])

    left, right = lax.fori_loop(0, groups, turn, (left, right))
    for q in range(groups):
        at = slice(8 * q, 8 * q + 8)
        upper = upper_ref[at, :]
        if q:
            upper = pltpu.roll(upper, 8 * q, 1)
        packed_ref[at, :] = jnp.where(lane < sub + 8 * q, left[q], upper)
        binv_ref[at, :] = right[q] * scale_ref[at, :]


def exchange_kernel(
    matrix, rows_ref, mask_ref, held, incoming_ref, returning_ref, packed_ref,
    other, upper_ref, scale_ref, arrive, depart, swap_sems,
):
    plane, chip = lax.axis_index("prow"), lax.axis_index("pcol")
    x, y, z = chip % 4, (chip // 4) % 4, chip // 16
    place = jnp.where(plane == 0, chip, (4 - x) % 4 + 4 * ((4 - y) % 4) + 16 * ((8 - z) % 8))
    bits = [(place // (2**i)) % 2 == 1 for i in range(7)]
    words = [pick(list(table), bits) for table in (TREES_A, TREES_B)]
    nodes = [(words[t // 3] // (2 ** (10 * (t % 3)))) % 1024 for t in range(TREES)]
    sends = [node % 64 for node in nodes]
    depths = [node // 64 for node in nodes]
    step = 1 - 2 * plane
    neighbours = []
    for sign in (step, -step):
        neighbours.append((
            (x + sign + 4) % 4 + 4 * y + 16 * z,
            x + 4 * ((y + sign + 4) % 4) + 16 * z,
            x + 4 * y + 16 * ((z + sign + 8) % 8),
        ))
    neighbours = [neighbours[d % 2][d // 2] for d in range(6)]
    root = chip == 0

    barrier = pltpu.get_barrier_semaphore()
    for there in neighbours:
        pl.semaphore_signal(barrier, inc=1, device_id=(plane, there), device_id_type=MESH)
    pl.semaphore_signal(barrier, inc=1, device_id=(1 - plane, chip), device_id_type=MESH)
    pl.semaphore_wait(barrier, 7)

    swap = pltpu.make_async_remote_copy(
        src_ref=rows_ref, dst_ref=other, send_sem=swap_sems.at[0], recv_sem=swap_sems.at[1],
        device_id=(1 - plane, chip), device_id_type=MESH,
    )
    swap.start()

    def piece(t, c):
        return pl.ds(pl.multiple_of(t * SPAN + c * PIECE, 8), PIECE)

    @pl.when(root)
    def _():
        for c in range(CHUNKS):
            for t in range(TREES):
                lo = t * SPAN + c * PIECE
                size = min(PIECE, EXT - lo)
                if size > 0:
                    pltpu.make_async_copy(
                        matrix.at[pl.ds(lo, size), pl.ds(0, NB)],
                        held.at[pl.ds(lo, size), :],
                        arrive.at[t, c],
                    ).start()

    def send(t, c, at):
        for d in range(6):
            @pl.when((sends[t] // (2**d)) % 2 == 1)
            def _():
                pltpu.make_async_remote_copy(
                    src_ref=held.at[at, :], dst_ref=held.at[at, :],
                    send_sem=depart.at[t, d], recv_sem=arrive.at[t, c],
                    device_id=(plane, neighbours[d]), device_id_type=MESH,
                ).start()

    def arrived(t, c, at):
        pltpu.make_async_copy(held.at[at, :], held.at[at, :], arrive.at[t, c]).wait()

    late = CHUNKS - 2

    def pass_on(s, carry):
        for t in range(TREES):
            c = s - depths[t]
            limit = CHUNKS
            if t == TREES - 1:
                limit = jnp.where(root, late, CHUNKS)

            @pl.when((c >= 0) & (c < limit))
            def _():
                at = piece(t, c)
                arrived(t, c, at)
                send(t, c, at)
        return carry

    lax.fori_loop(0, jnp.where(root, CHUNKS, DEEPEST + CHUNKS), pass_on, 0)

    swap.wait()
    mine = jnp.concatenate([mask_ref[...]] * (matrix.shape[1] // NB), axis=1) > 0.5
    incoming_ref[...] = jnp.where(mine, rows_ref[:NB, :], other[:NB, :])
    returning_ref[...] = jnp.where(plane == 0, rows_ref[NB:, :], other[NB:, :])

    @pl.when(root)
    def _():
        t, lo = TREES - 1, (TREES - 1) * SPAN + late * PIECE
        part = pl.ds(lo, EXT - lo)
        pltpu.make_async_copy(held.at[part, :], held.at[part, :], arrive.at[t, late]).wait()
        held[EXT : EXT + FEW, :] = returning_ref[:, :NB]
        held[EXT + FEW : INV, :] = jnp.zeros((INV - EXT - FEW, NB), F32)
        for c in range(late, CHUNKS):
            send(t, c, pl.ds(t * SPAN + c * PIECE, PIECE))
        eliminate(
            incoming_ref[:, :NB], packed_ref,
            held.at[INV : INV + NB, :], held.at[INV + NB : INV + 2 * NB, :],
            upper_ref, scale_ref,
        )
        held[INV + 2 * NB : HELD, :] = jnp.zeros((HELD - INV - 2 * NB, NB), F32)

    def pass_tail(s, carry):
        for t in range(TREES):
            @pl.when(depths[t] == s)
            def _():
                at = pl.ds(INV + t * TAIL, TAIL)

                @pl.when(s > 0)
                def _():
                    arrived(t, CHUNKS, at)
                send(t, CHUNKS, at)
        return carry

    lax.fori_loop(0, jnp.where(root, 1, DEEPEST + 1), pass_tail, 0)

    for t in range(TREES):
        for d in range(6):
            @pl.when((sends[t] // (2**d)) % 2 == 1)
            def _():
                at = pl.ds(0, SPAN + TAIL)
                pltpu.make_async_copy(held.at[at, :], held.at[at, :], depart.at[t, d]).wait()


def exchange(matrix, rows, mask):
    cols = matrix.shape[1]
    vmem = pl.BlockSpec(memory_space=pltpu.VMEM)
    return pl.pallas_call(
        exchange_kernel,
        name="exchange",
        out_shape=(
            jax.ShapeDtypeStruct((HELD, NB), F32),
            jax.ShapeDtypeStruct((NB, cols), F32),
            jax.ShapeDtypeStruct((FEW, cols), F32),
            jax.ShapeDtypeStruct((NB, NB), F32),
        ),
        in_specs=[pl.BlockSpec(memory_space=pl.ANY), vmem, vmem],
        out_specs=(vmem,) * 4,
        scratch_shapes=[
            pltpu.VMEM((NB + FEW, cols), F32),
            pltpu.VMEM((NB, NB), F32),
            pltpu.VMEM((NB, NB), F32),
            pltpu.SemaphoreType.DMA((TREES, CHUNKS + 1)),
            pltpu.SemaphoreType.DMA((TREES, 6)),
            pltpu.SemaphoreType.DMA((2,)),
        ],
        compiler_params=pltpu.CompilerParams(
            collective_id=0, has_side_effects=True, vmem_limit_bytes=24 * 2**20
        ),
    )(matrix, rows, mask)


TILE = 512


def update_kernel(
    tab, tile_ref, panel_ref, ext_ref, linv_ref, binv_ref, incoming_ref, returning_ref, packed_ref, out_ref,
    right, patch, top,
):
    j = pl.program_id(0)
    plane, first = lax.axis_index("prow"), lax.axis_index("pcol") == 0

    def product(left_f32):
        high = left_f32.astype(BF16)
        low = (left_f32 - high.astype(F32)).astype(BF16)
        return jnp.dot(
            jnp.concatenate([high, high, low], axis=1), right[...], preferred_element_type=F32
        )

    def keep(block):
        return jnp.concatenate([jnp.where(first, 0.0, block[:, :NB]), block[:, NB:]], axis=1)

    @pl.when(j == 0)
    def _():
        source = incoming_ref[...]
        top[...] = jnp.dot(linv_ref[...], source, precision=HIGH, preferred_element_type=F32)
        lane = lax.broadcasted_iota(I32, (NB, NB), 1)
        sub = lax.broadcasted_iota(I32, (NB, NB), 0)
        packed = packed_ref[...]
        unit = jnp.where(lane < sub, packed, jnp.where(lane == sub, 1.0, 0.0))

        @pl.when(first)
        def _():
            top[:, :NB] = packed
        source = jnp.concatenate([jnp.where(first, -unit, source[:, :NB]), source[:, NB:]], axis=1)
        w = jnp.dot(binv_ref[...], source, precision=HIGH, preferred_element_type=F32)
        high = w.astype(BF16)
        right[0:NB, :] = high
        right[NB : 2 * NB, :] = (w - high.astype(F32)).astype(BF16)
        right[2 * NB :, :] = high
        patch[...] = keep(returning_ref[...]) - product(ext_ref[0:FEW, :])

    out_ref[...] = keep(tile_ref[...]) - product(panel_ref[...])

    @pl.when((j == 0) & (plane == 0))
    def _():
        out_ref[0:NB, :] = top[...]

    base = plane * 4096 + j * TILE

    def land(i, carry):
        out_ref[pl.ds(tab[0, i] - base, 1), :] = patch[pl.ds(i, 1), :]
        return carry

    lax.fori_loop(tab[2, j], tab[2, j + 1], land, 0)


def update(matrix, held, incoming, returning, packed, tab):
    rows, cols = matrix.shape
    vmem = pl.BlockSpec(memory_space=pltpu.VMEM)
    whole = lambda shape: pl.BlockSpec(shape, lambda j: (0, 0))
    return pl.pallas_call(
        update_kernel,
        name="update",
        grid=(rows // TILE,),
        out_shape=jax.ShapeDtypeStruct((rows, cols), F32),
        in_specs=[
            pl.BlockSpec(memory_space=pltpu.SMEM),
            pl.BlockSpec((TILE, cols), lambda j: (j, 0)),
            pl.BlockSpec((TILE, NB), lambda j: (j, 0)),
            pl.BlockSpec((NB, NB), lambda j: (EXT // NB, 0)),
            pl.BlockSpec((NB, NB), lambda j: (INV // NB, 0)),
            pl.BlockSpec((NB, NB), lambda j: (INV // NB + 1, 0)),
            whole((NB, cols)), whole((FEW, cols)), whole((NB, NB)),
        ],
        out_specs=pl.BlockSpec((TILE, cols), lambda j: (j, 0)),
        scratch_shapes=[
            pltpu.VMEM((3 * NB, cols), BF16),
            pltpu.VMEM((FEW, cols), F32),
            pltpu.VMEM((NB, cols), F32),
        ],
        compiler_params=pltpu.CompilerParams(vmem_limit_bytes=24 * 2**20),
    )(tab, matrix, held, held, held, held, incoming, returning, packed)


def on_device(matrix, pivot_rows):
    rows, mask, tab = gather(matrix, pivot_rows)
    held, incoming, returning, packed = exchange(matrix, rows, mask)
    return update(matrix, held, incoming, returning, packed, tab)


def solution(mesh):
    return jax.shard_map(
        on_device, mesh=mesh, in_specs=(P("prow", "pcol"), P()), out_specs=P("prow", "pcol"), check_vma=False
    )
```

time: 617 us -> 104 us (0.17)
  the two profiles are of different devices: /device:TPU:2 before, /device:TPU:52 now
where the time goes in v1:
time: 104 us
  Pallas kernels  99 us (95%)
  local copies, waits for them, and re-layouts  4.6 us (4%)
    pallas_call x1, Pallas kernels, exchange(): pl.pallas_call(exchange_kernel, name='exchange', out_shape=(jax.ShapeDtyp...  86.9 us
    pallas_call x1, Pallas kernels, update(): pl.pallas_call(update_kernel, name='update', grid=(rows // TILE,), out_sh...  7.39 us
    pallas_call x1, Pallas kernels, gather(): pl.pallas_call(gather_kernel, name='gather_rows', out_shape=(jax.ShapeDty...  4.74 us
    unnamed x8, local copies, waits for them, and re-layouts  4.6 us

profile of v1, /device:TPU:52, one launch (start us, length us, event | category | flops | bytes accessed | tf_op | source)
XLA Modules:
  0.0 103.6 jit_solution(6323947712995771552)
XLA Ops:
  0.0 4.7 %gather_rows.1 = (f32[224,384]{1,0:T(8,128)}, f32[128,128]{1,0:T(8,128)}, s32[8,128]{1,0:T(8,128)}) custom-call(s32[128]{0:T(128)} %pivots_sm.1, s32[1,128]{1,0:T(1,128)} %bitcast.1, f32[4096,384]{1,0:T(8,128)} %tile_ref.1), custom_call_target="tpu_custom_call" | custom-call | tf_op jit(solution)/shard_map/gather_rows/pallas_call | solution.py:128
  4.7 0.0 copy-start.3
  4.8 0.0 copy-start
  4.8 2.8 %copy-done = f32[4096,384]{1,0:T(8,128)S(1)} copy-done((f32[4096,384]{1,0:T(8,128)S(1)}, f32[4096,384]{1,0:T(8,128)}, u32[]{:S(2)}) %copy-start) | copy-done | bytes 6291480
  7.5 0.0 copy-start.1
  7.5 1.0 copy-done.1
  8.5 0.0 copy-start.2
  8.5 0.8 copy-done.2
  9.4 86.9 %exchange.1 = (f32[4512,128]{1,0:T(8,128)S(1)}, f32[128,384]{1,0:T(8,128)S(1)}, f32[96,384]{1,0:T(8,128)S(1)}, f32[128,128]{1,0:T(8,128)S(1)}) custom-call(f32[4096,384]{1,0:T(8,128)S(1)} %copy-done, f32[224,384]{1,0:T(8,128)S(1)} %copy-done.1, f32[128,128]{1,0:T(8,128)S(1)} %copy-done.2), custom_call_target="tpu_custom_call" | custom-call | tf_op jit(solution)/shard_map/exchange/pallas_call | solution.py:337
  96.2 0.0 copy-done.3
  96.2 7.4 %update.1 = f32[4096,384]{1,0:T(8,128)} custom-call(s32[8,128]{1,0:T(8,128)S(1)} %copy-done.3, f32[4096,384]{1,0:T(8,128)S(1)} %copy-done, f32[4512,128]{1,0:T(8,128)S(1)} %get-tuple-element.15.panel_ref.ext_ref.linv_ref.binv_ref, f32[4512,128]{1,0:T(8,128)S(1)} %get-tuple-element.15.panel_ref.ext_ref.linv_ref.binv_ref, ...), custom_call_target="tpu_custom_call" | custom-call | tf_op jit(solution)/shard_map/update/pallas_call | solution.py:421
Async XLA Ops:
  4.7 91.5 %copy-start.3 = (s32[8,128]{1,0:T(8,128)S(1)}, s32[8,128]{1,0:T(8,128)}, u32[]{:S(2)}) copy-start(s32[8,128]{1,0:T(8,128)} %get-tuple-element.12.tab) | copy-start | bytes 12292
  4.8 2.8 %copy-start = (f32[4096,384]{1,0:T(8,128)S(1)}, f32[4096,384]{1,0:T(8,128)}, u32[]{:S(2)}) copy-start(f32[4096,384]{1,0:T(8,128)} %tile_ref.1) | copy-start | bytes 18874372
  7.5 1.0 copy-start.1
  8.5 0.8 copy-start.2

commit v2 on v1

v2 whole, which is shorter than its diff:
```python
import functools

import jax
import jax.numpy as jnp
from jax import lax
from jax.experimental import pallas as pl
from jax.experimental.pallas import tpu as pltpu
from jax.sharding import PartitionSpec as P

NB = 128
FEW = 96
F32 = jnp.float32
BF16 = jnp.bfloat16
I32 = jnp.int32
HIGH = lax.Precision.HIGHEST
MESH = pl.DeviceIdType.MESH

HOPS = (
    (1, 0, 0), (3, 0, 0), (2, 0, 0), (0, 1, 0), (0, 3, 0), (0, 2, 0),
    (0, 0, 1), (0, 0, 7), (0, 0, 2), (0, 0, 6), (0, 0, 3), (0, 0, 5), (0, 0, 4),
)
PANEL_TREES = (
    (
        768, 0, 0, 0, 0, 0, 0, 0, 0, 0,
        0, 0, 0, 0, 0, 98313, 49160, 73745, 90240, 0,
        73737, 90241, 0, 90264, 90240, 98433, 0, 0, 73730, 90240,
        0, 90114, 24723, 49337, 73744, 49224, 0, 0, 90184, 73923,
        0, 73920, 0, 0, 49298, 73792, 0, 74320, 0, 0,
        0, 73731, 0, 0, 0, 90177, 0, 98323, 0, 0,
        0, 90178, 0, 90194, 0, 90242, 98305, 0, 0, 0,
        0, 0, 98312, 0, 0, 0, 0, 0, 0, 0,
        49155, 73864, 73880, 0, 98432, 90240, 98432, 0, 73881, 98440,
        0, 98448, 0, 0, 98449, 0, 24804, 0, 57592, 0,
        0, 0, 73795, 98320, 57547, 0, 82688, 73920, 0, 98312,
        73795, 0, 49169, 73800, 73729, 0, 98496, 0, 98377, 0,
        73745, 0, 0, 98368, 0, 0, 98371, 0,
    ),
    (
        264, 0, 0, 0, 26757, 0, 49736, 0, 0, 90120,
        73738, 0, 0, 0, 90120, 0, 49169, 73880, 90176, 0,
        0, 0, 73852, 0, 90240, 0, 90176, 98432, 73872, 0,
        0, 90240, 24963, 49160, 0, 49328, 0, 73802, 0, 98432,
        0, 90248, 0, 73937, 0, 0, 90176, 73859, 73752, 0,
        0, 98306, 0, 90137, 0, 0, 0, 0, 0, 98323,
        0, 0, 0, 0, 57502, 0, 81952, 73872, 73729, 98305,
        0, 0, 0, 0, 0, 0, 73793, 98520, 0, 98434,
        73793, 0, 0, 0, 57375, 0, 81968, 73880, 73921, 98305,
        0, 98432, 98370, 0, 0, 0, 0, 0, 98306, 0,
        0, 98306, 73818, 90128, 0, 0, 98313, 0, 0, 0,
        0, 0, 65537, 90113, 0, 90176, 41011, 65544, 0, 65752,
        0, 90241, 0, 90113, 73731, 90241, 0, 90240,
    ),
    (
        17, 25608, 0, 0, 0, 45257, 65553, 90128, 0, 65537,
        0, 65601, 27143, 0, 53312, 41360, 0, 0, 90114, 0,
        90264, 65611, 0, 0, 0, 90113, 0, 90128, 0, 0,
        73803, 90121, 0, 0, 0, 90115, 0, 90115, 0, 0,
        0, 0, 0, 90131, 0, 0, 90114, 73816, 0, 57496,
        0, 0, 98306, 73739, 98320, 0, 0, 98432, 0, 0,
        98456, 73729, 98320, 90136, 0, 0, 0, 0, 0, 81940,
        0, 0, 98306, 0, 0, 0, 73880, 0, 90171, 0,
        73730, 0, 0, 98432, 98432, 0, 0, 0, 73746, 98448,
        0, 98320, 57497, 73816, 98329, 0, 0, 0, 98305, 0,
        90114, 90113, 0, 0, 73746, 0, 98368, 0, 49244, 98328,
        73881, 0, 0, 90129, 0, 0, 0, 65691, 90624, 0,
        0, 0, 0, 90129, 73736, 0, 0, 65562,
    ),
    (
        2049, 24625, 41160, 0, 0, 0, 65793, 90192, 73744, 49619,
        73921, 90120, 65600, 41218, 0, 0, 0, 0, 65561, 0,
        0, 90128, 0, 0, 90128, 73746, 90113, 0, 90121, 0,
        90241, 0, 0, 0, 0, 0, 0, 98320, 90177, 0,
        98320, 73811, 98369, 0, 90120, 73795, 90121, 0, 0, 0,
        0, 98432, 0, 0, 0, 0, 0, 98306, 0, 0,
        0, 90123, 0, 0, 57474, 0, 98496, 73930, 73864, 98456,
        0, 98442, 98312, 0, 0, 0, 0, 98305, 0, 98432,
        33016, 0, 0, 0, 57539, 73936, 0, 73792, 57414, 0,
        90320, 82496, 57411, 73937, 0, 73920, 57346, 0, 90120, 73792,
        73792, 0, 0, 98368, 0, 0, 0, 0, 73792, 98329,
        0, 0, 0, 90130, 65682, 0, 0, 90113, 0, 0,
        0, 73746, 90113, 0, 0, 0, 90113, 0,
    ),
    (
        545, 25808, 0, 0, 0, 0, 73792, 73793, 24838, 0,
        59536, 49168, 0, 40977, 65537, 90120, 0, 40979, 65680, 0,
        0, 0, 98312, 90129, 0, 90128, 0, 98312, 90240, 65554,
        0, 0, 0, 73739, 98305, 0, 0, 0, 0, 98368,
        57538, 0, 98322, 73946, 0, 98307, 0, 0, 0, 57563,
        73809, 0, 98432, 73729, 0, 0, 73744, 0, 0, 0,
        0, 73872, 98321, 0, 0, 73738, 98320, 0, 0, 98376,
        0, 98395, 0, 0, 0, 0, 90258, 0, 0, 0,
        90114, 0, 0, 0, 73744, 0, 0, 0, 0, 0,
        90259, 0, 73873, 90249, 0, 0, 24600, 65537, 90256, 0,
        49283, 0, 0, 74264, 73792, 0, 98322, 0, 49299, 0,
        0, 73920, 65546, 41098, 0, 0, 0, 65600, 98320, 0,
        0, 98312, 73883, 98320, 0, 0, 0, 90113,
    ),
    (
        34, 65544, 40978, 27658, 0, 90120, 0, 41153, 28864, 0,
        0, 90240, 0, 0, 65553, 0, 0, 98314, 0, 90128,
        0, 0, 0, 65617, 49163, 73824, 90128, 73858, 73729, 90113,
        0, 0, 0, 0, 98434, 73745, 0, 0, 0, 90113,
        0, 90139, 0, 0, 0, 0, 0, 0, 0, 98320,
        73858, 57499, 98305, 0, 98496, 73731, 0, 0, 0, 98432,
        98432, 0, 98432, 73747, 0, 0, 98306, 73738, 90192, 0,
        0, 0, 65749, 90328, 90249, 0, 0, 0, 0, 98305,
        0, 98376, 73818, 57554, 0, 0, 98369, 0, 0, 0,
        0, 98306, 98312, 0, 98370, 73937, 0, 0, 0, 73729,
        90114, 0, 0, 0, 73747, 90129, 0, 0, 90113, 0,
        0, 98368, 0, 0, 0, 0, 0, 90114, 90200, 65554,
        49289, 73744, 0, 0, 73929, 90185, 0, 0,
    ),
)
TAIL_TREES = (
    (
        1588, 0, 63496, 0, 0, 139328, 98369, 0, 61457, 98712,
        0, 131202, 43202, 139272, 0, 90392, 0, 0, 0, 0,
        0, 0, 139329, 0, 131104, 0, 0, 0, 90134, 0,
        139418, 131096, 0, 147585, 0, 0, 147600, 0, 0, 0,
        0, 147611, 0, 0, 0, 0, 0, 139291, 65579, 106713,
        0, 106584, 106688, 0, 0, 147650, 122884, 0, 0, 0,
        0, 147475, 0, 147472, 0, 147480, 131128, 0, 147536, 0,
        0, 0, 131147, 0, 0, 0, 0, 0, 0, 0,
        0, 0, 122914, 0, 0, 0, 0, 0, 0, 0,
        0, 0, 106507, 147472, 0, 147610, 57356, 0, 106587, 0,
        98315, 139392, 147648, 139456, 139338, 0, 0, 0, 0, 0,
        147473, 0, 131080, 0, 147475, 0, 0, 0, 0, 0,
        0, 139409, 0, 0, 90123, 131200, 0, 0,
    ),
    (
        313, 44160, 0, 0, 43012, 0, 102913, 139328, 61572, 0,
        109642, 0, 45568, 0, 0, 0, 98315, 139272, 147584, 139392,
        0, 0, 0, 0, 147464, 0, 147483, 0, 0, 0,
        0, 0, 57767, 98328, 106632, 98328, 0, 139266, 147528, 139336,
        106688, 0, 0, 0, 0, 139411, 0, 139456, 0, 106585,
        147472, 0, 0, 147458, 0, 0, 147466, 0, 0, 0,
        0, 147472, 0, 0, 106626, 147472, 0, 147586, 0, 0,
        0, 0, 131095, 0, 0, 0, 122886, 0, 0, 0,
        0, 106587, 147464, 0, 106506, 147648, 0, 147600, 147466, 0,
        0, 0, 0, 147473, 0, 0, 0, 147458, 0, 0,
        0, 0, 147481, 0, 139281, 0, 0, 0, 98322, 0,
        0, 139674, 131088, 90139, 131081, 0, 0, 131138, 0, 0,
        98307, 0, 0, 139354, 0, 131265, 0, 0,
    ),
    (
        2311, 45584, 62472, 41136, 0, 0, 98498, 139265, 0, 0,
        0, 102417, 0, 90320, 131088, 90626, 98354, 0, 0, 0,
        139267, 0, 139288, 0, 0, 0, 0, 0, 0, 131101,
        0, 0, 57528, 0, 0, 0, 98435, 139328, 0, 139346,
        106499, 147521, 0, 147648, 98883, 139337, 0, 0, 0, 0,
        123049, 0, 0, 0, 0, 0, 0, 0, 0, 0,
        139294, 0, 0, 0, 106512, 123044, 131192, 0, 147587, 0,
        0, 0, 0, 0, 0, 0, 147473, 0, 0, 0,
        65722, 0, 0, 106568, 106689, 147465, 0, 0, 122884, 0,
        0, 0, 106499, 147464, 0, 147602, 0, 98353, 139272, 147465,
        147520, 0, 0, 0, 0, 147475, 0, 0, 0, 139267,
        0, 139280, 0, 0, 0, 90163, 0, 0, 139274, 0,
        0, 0, 0, 139265, 0, 131098, 0, 131106,
    ),
)
SPREAD = 12
TAIL_SPREAD = 18

TREES = len(PANEL_TREES)
TAILS = len(TAIL_TREES)
CHUNKS = 11
PIECE = 64
SPAN = PIECE * CHUNKS
LATE = 9
EXT = 4096
INV = TREES * SPAN
TAIL = -(-2 * NB // (8 * TAILS)) * 8
HELD = INV + TAILS * TAIL
TILE = 512


def swap_lists(pivot_col, pivot_row, row_start, tab_ref):
    lane = lax.broadcasted_iota(I32, (NB, NB), 1)
    sub = lax.broadcasted_iota(I32, (NB, NB), 0)
    low = pivot_col >= NB
    smaller = (pivot_row < pivot_col) & (pivot_row >= NB)
    rank = jnp.sum(jnp.where(smaller, 1.0, 0.0), axis=1, keepdims=True)
    lane_f = lane.astype(F32)
    hit = (rank == lane_f) & low
    landing = jnp.sum(jnp.where(hit, pivot_col.astype(F32), 0.0), axis=0, keepdims=True)
    chosen = jnp.sum(jnp.where(pivot_col == lane, 1.0, 0.0), axis=0, keepdims=True)
    free = jnp.broadcast_to(1.0 - chosen, (NB, NB))
    ahead = jnp.sum(jnp.where(lane < sub, free, 0.0), axis=1, keepdims=True)
    own = jnp.sum(jnp.where(lane == sub, free, 0.0), axis=1, keepdims=True)
    place = (ahead == lane_f) & (own > 0.5)
    displaced = jnp.sum(jnp.where(place, sub.astype(F32), 0.0), axis=0, keepdims=True)
    bound = row_start + lane * TILE
    starts = jnp.sum(jnp.where(low & (pivot_col < bound), 1.0, 0.0), axis=0, keepdims=True)
    tab_ref[...] = jnp.concatenate(
        [landing, displaced, starts, jnp.zeros((5, NB), F32)], axis=0
    ).astype(I32)


def pick(values, bits):
    while len(values) > 1:
        bit, bits = bits[0], bits[1:]
        values = [
            lo if isinstance(lo, int) and isinstance(hi, int) and lo == hi else jnp.where(bit, hi, lo)
            for lo, hi in zip(values[::2], values[1::2])
        ]
    return values[0]


def eliminate(block, packed_ref, linv_ref, binv_ref, upper_ref, scale_ref):
    lane = lax.broadcasted_iota(I32, (8, NB), 1)
    sub = lax.broadcasted_iota(I32, (8, NB), 0)
    groups = NB // 8
    left = tuple(block[8 * q : 8 * q + 8, :] for q in range(groups))
    right = tuple(jnp.where(lane == sub + 8 * q, 1.0, 0.0) for q in range(groups))

    def row_of(x, k):
        return jnp.broadcast_to(x[k : k + 1, :], (8, NB))

    def column_of(x, k):
        return jnp.broadcast_to(x[:, k : k + 1], (8, NB))

    def turn(g, carry):
        a, z = list(carry[0]), list(carry[1])
        active = lane < NB - 8 * g
        upper, linv, scale = a[0], z[0], jnp.zeros((8, NB), F32)
        column = [column_of(a[0], j) for j in range(8)]
        for k in range(8):
            pivot = row_of(column[k], k)
            row_a, row_z = row_of(a[0], k), row_of(z[0], k)
            inverse = 1.0 / pivot
            here = sub == k
            upper = jnp.where(here, row_a, upper)
            linv = jnp.where(here, row_z, linv)
            scale = jnp.where(here, inverse, scale)
            row_a = jnp.where(
                lane > k, jnp.where(active, row_a, 0.0), jnp.where(lane == k, pivot - 1.0, 0.0)
            )
            first = jnp.where(here, 0.0, column[k] * inverse)
            for j in range(k + 1, 8):
                column[j] = column[j] - first * row_of(column[j], k)
            for q in range(groups):
                factor = first if q == 0 else column_of(a[q], k) * inverse
                a[q] = a[q] - factor * row_a
                z[q] = z[q] - factor * row_z
        at = pl.ds(pl.multiple_of(8 * g, 8), 8)
        upper_ref[at, :] = upper
        linv_ref[at, :] = linv
        scale_ref[at, :] = scale
        a = [pltpu.roll(x, NB - 8, 1) for x in a]
        return tuple(a[1:] + a[:1]), tuple(z[1:] + z[:1])

    left, right = lax.fori_loop(0, groups, turn, (left, right))
    for q in range(groups):
        at = slice(8 * q, 8 * q + 8)
        upper = upper_ref[at, :]
        if q:
            upper = pltpu.roll(upper, 8 * q, 1)
        packed_ref[at, :] = jnp.where(lane < sub + 8 * q, left[q], upper)
        binv_ref[at, :] = right[q] * scale_ref[at, :]


def exchange_kernel(
    pivots_sm, pivots_v, matrix, tile_ref, held, incoming_ref, returning_ref, packed_ref, tab_ref,
    rows_ref, other, upper_ref, scale_ref, tab_sm,
    arrive, depart, tail_arrive, tail_depart, swap_sems, local_sems,
):
    plane, chip = lax.axis_index("prow"), lax.axis_index("pcol")
    rows_dev, cols = matrix.shape
    row_start = plane * rows_dev
    root = chip == 0

    @pl.when(root)
    def _():
        for c in range(CHUNKS):
            for t in range(TREES):
                lo = t * SPAN + c * PIECE
                if lo < EXT:
                    pltpu.make_async_copy(
                        matrix.at[pl.ds(lo, PIECE), pl.ds(0, NB)],
                        held.at[pl.ds(lo, PIECE), :],
                        arrive.at[t, c],
                    ).start()
    load = pltpu.make_async_copy(matrix, tile_ref, local_sems.at[0])
    load.start()

    x, y, z = chip % 4, (chip // 4) % 4, chip // 16
    axis_chips = [(x + dx) % 4 + 4 * ((y + dy) % 4) + 16 * ((z + dz) % 8) for dx, dy, dz in HOPS]
    barrier = pltpu.get_barrier_semaphore()
    for there in axis_chips:
        pl.semaphore_signal(barrier, inc=1, device_id=(plane, there), device_id_type=MESH)
    pl.semaphore_signal(barrier, inc=1, device_id=(1 - plane, chip), device_id_type=MESH)

    place = jnp.where(plane == 0, chip, (4 - x) % 4 + 4 * ((4 - y) % 4) + 16 * ((8 - z) % 8))
    bits = [(place // (2**i)) % 2 == 1 for i in range(7)]
    full = 2 ** len(HOPS)
    words = [pick(list(table), bits) for table in PANEL_TREES]
    sends, turns = [w % full for w in words], [w // full for w in words]
    words = [pick(list(table), bits) for table in TAIL_TREES]
    tail_sends, tail_turns = [w % full for w in words], [w // full for w in words]
    mirrored = [HOPS.index(((4 - dx) % 4, (4 - dy) % 4, (8 - dz) % 8)) for dx, dy, dz in HOPS]
    targets = [
        jnp.where(plane == 0, axis_chips[d], axis_chips[mirrored[d]]) for d in range(len(HOPS))
    ]

    pivot_row = jnp.broadcast_to(pivots_v[...], (NB, NB))
    pivot_col = jnp.transpose(pivot_row.astype(F32)).astype(I32)
    swap_lists(pivot_col, pivot_row, row_start, tab_ref)
    move = pltpu.make_async_copy(tab_ref, tab_sm, local_sems.at[1])
    move.start()
    mine = (pivot_col >= row_start) & (pivot_col < row_start + rows_dev)

    pl.semaphore_wait(barrier, len(HOPS) + 1)

    def send(mask, at, out_sems, in_sem):
        for d in range(len(HOPS)):
            @pl.when((mask // (2**d)) % 2 == 1)
            def _():
                pltpu.make_async_remote_copy(
                    src_ref=held.at[at, :], dst_ref=held.at[at, :],
                    send_sem=out_sems.at[d], recv_sem=in_sem,
                    device_id=(plane, targets[d]), device_id_type=MESH,
                ).start()

    def arrived(at, sem):
        pltpu.make_async_copy(held.at[at, :], held.at[at, :], sem).wait()

    def pass_on(s, carry):
        for t in range(TREES):
            c = s - turns[t]
            limit = CHUNKS
            if t == TREES - 1:
                limit = jnp.where(root, LATE, CHUNKS)

            @pl.when((c >= 0) & (c < limit) & (sends[t] > 0))
            def _():
                at = pl.ds(pl.multiple_of(t * SPAN + c * PIECE, 8), PIECE)
                arrived(at, arrive.at[t, c])
                send(sends[t], at, depart.at[t], arrive.at[t, c])
        return carry

    @pl.when(root)
    def _():
        lax.fori_loop(0, CHUNKS, pass_on, 0)

    load.wait()
    move.wait()

    def first(i, carry):
        for j in range(8):
            k = 8 * i + j
            local = jnp.clip(pivots_sm[k] - row_start, 0, rows_dev - 1)
            rows_ref[pl.ds(k, 1), :] = tile_ref[pl.ds(local, 1), :]
        return carry

    lax.fori_loop(0, NB // 8, first, 0)

    def second(i, carry):
        for j in range(8):
            k = 8 * i + j
            local = jnp.clip(tab_sm[1, k], 0, NB - 1)
            rows_ref[pl.ds(NB + k, 1), :] = tile_ref[pl.ds(local, 1), :]
        return carry

    lax.fori_loop(0, FEW // 8, second, 0)

    swaps = []
    for i, part in enumerate((pl.ds(0, NB), pl.ds(NB, cols - NB))):
        swaps.append(pltpu.make_async_remote_copy(
            src_ref=rows_ref.at[:, part], dst_ref=other.at[:, part],
            send_sem=swap_sems.at[i, 0], recv_sem=swap_sems.at[i, 1],
            device_id=(1 - plane, chip), device_id_type=MESH,
        ))
        swaps[i].start()

    @pl.when(chip != 0)
    def _():
        lax.fori_loop(0, SPREAD + CHUNKS, pass_on, 0)

    for i, swap in enumerate(swaps):
        swap.wait()
        for j in range(1 if i == 0 else cols // NB - 1):
            at = slice((i + j) * NB, (i + j + 1) * NB)
            incoming_ref[:, at] = jnp.where(mine, rows_ref[:NB, at], other[:NB, at])
            returning_ref[:, at] = jnp.where(plane == 0, rows_ref[NB:, at], other[NB:, at])
        if i == 0:
            @pl.when(root)
            def _():
                held[EXT : EXT + FEW, :] = returning_ref[:, :NB]
                held[EXT + FEW : INV, :] = jnp.zeros((INV - EXT - FEW, NB), F32)
                t = TREES - 1
                for c in range(LATE, CHUNKS):
                    send(sends[t], pl.ds(t * SPAN + c * PIECE, PIECE), depart.at[t], arrive.at[t, c])
                eliminate(
                    incoming_ref[:, :NB], packed_ref,
                    held.at[INV : INV + NB, :], held.at[INV + NB : INV + 2 * NB, :],
                    upper_ref, scale_ref,
                )
                if HELD > INV + 2 * NB:
                    held[INV + 2 * NB : HELD, :] = jnp.zeros((HELD - INV - 2 * NB, NB), F32)

    def pass_tail(s, carry):
        for t in range(TAILS):
            @pl.when((tail_turns[t] == s) & (tail_sends[t] > 0))
            def _():
                at = pl.ds(INV + t * TAIL, TAIL)

                @pl.when(chip != 0)
                def _():
                    arrived(at, tail_arrive.at[t])
                send(tail_sends[t], at, tail_depart.at[t], tail_arrive.at[t])
        return carry

    lax.fori_loop(0, jnp.where(root, 1, TAIL_SPREAD + 1), pass_tail, 0)

    for t in range(TREES):
        @pl.when((chip != 0) & (sends[t] == 0))
        def _():
            for c in range(CHUNKS):
                arrived(pl.ds(t * SPAN + c * PIECE, PIECE), arrive.at[t, c])
    for t in range(TAILS):
        @pl.when((chip != 0) & (tail_sends[t] == 0))
        def _():
            arrived(pl.ds(INV + t * TAIL, TAIL), tail_arrive.at[t])
    for trees, masks, sems, size in (
        (TREES, sends, depart, SPAN), (TAILS, tail_sends, tail_depart, TAIL)
    ):
        for t in range(trees):
            for d in range(len(HOPS)):
                @pl.when((masks[t] // (2**d)) % 2 == 1)
                def _():
                    arrived(pl.ds(0, size), sems.at[t, d])


def exchange(matrix, pivot_rows):
    rows, cols = matrix.shape
    vmem = pl.BlockSpec(memory_space=pltpu.VMEM)
    return pl.pallas_call(
        exchange_kernel,
        name="exchange",
        out_shape=(
            jax.ShapeDtypeStruct((rows, cols), F32),
            jax.ShapeDtypeStruct((HELD, NB), F32),
            jax.ShapeDtypeStruct((NB, cols), F32),
            jax.ShapeDtypeStruct((FEW, cols), F32),
            jax.ShapeDtypeStruct((NB, NB), F32),
            jax.ShapeDtypeStruct((8, NB), I32),
        ),
        in_specs=[
            pl.BlockSpec(memory_space=pltpu.SMEM), vmem, pl.BlockSpec(memory_space=pltpu.HBM),
        ],
        out_specs=(vmem,) * 6,
        scratch_shapes=[
            pltpu.VMEM((NB + FEW, cols), F32),
            pltpu.VMEM((NB + FEW, cols), F32),
            pltpu.VMEM((NB, NB), F32),
            pltpu.VMEM((NB, NB), F32),
            pltpu.SMEM((8, NB), I32),
            pltpu.SemaphoreType.DMA((TREES, CHUNKS)),
            pltpu.SemaphoreType.DMA((TREES, len(HOPS))),
            pltpu.SemaphoreType.DMA((TAILS,)),
            pltpu.SemaphoreType.DMA((TAILS, len(HOPS))),
            pltpu.SemaphoreType.DMA((2, 2)),
            pltpu.SemaphoreType.DMA((2,)),
        ],
        compiler_params=pltpu.CompilerParams(
            collective_id=0, has_side_effects=True, vmem_limit_bytes=44 * 2**20
        ),
    )(pivot_rows, pivot_rows.reshape(1, NB), matrix)


SLOTS = 3


def update_kernel(
    tab, tile_ref, held, incoming_ref, returning_ref, packed_ref, out_ref,
    slots, right, patch, sems,
):
    plane, first = lax.axis_index("prow"), lax.axis_index("pcol") == 0
    rows = tile_ref.shape[0]

    def product(left_f32):
        high = left_f32.astype(BF16)
        low = (left_f32 - high.astype(F32)).astype(BF16)
        return jnp.dot(
            jnp.concatenate([high, high, low], axis=1), right[...], preferred_element_type=F32
        )

    def keep(block):
        return jnp.concatenate([jnp.where(first, 0.0, block[:, :NB]), block[:, NB:]], axis=1)

    source = incoming_ref[...]
    lane = lax.broadcasted_iota(I32, (NB, NB), 1)
    sub = lax.broadcasted_iota(I32, (NB, NB), 0)
    packed = packed_ref[...]
    unit = jnp.where(lane < sub, packed, jnp.where(lane == sub, 1.0, 0.0))
    w = jnp.dot(
        held[INV + NB : INV + 2 * NB, :],
        jnp.concatenate([jnp.where(first, -unit, source[:, :NB]), source[:, NB:]], axis=1),
        precision=HIGH, preferred_element_type=F32,
    )
    high = w.astype(BF16)
    right[0:NB, :] = high
    right[NB : 2 * NB, :] = (w - high.astype(F32)).astype(BF16)
    right[2 * NB :, :] = high
    patch[...] = keep(returning_ref[...]) - product(held[EXT : EXT + FEW, :])

    copies = []
    for j in range(rows // TILE):
        slot = slots.at[j % SLOTS]
        if j >= SLOTS:
            copies[j - SLOTS].wait()
        at = slice(j * TILE, (j + 1) * TILE)
        slot[...] = keep(tile_ref[at, :]) - product(held[at, :])
        if j == 0:
            @pl.when(plane == 0)
            def _():
                upper = jnp.dot(
                    held[INV : INV + NB, :], source, precision=HIGH, preferred_element_type=F32
                )
                slot[0:NB, :] = jnp.concatenate(
                    [jnp.where(first, packed, upper[:, :NB]), upper[:, NB:]], axis=1
                )
        base = plane * rows + j * TILE

        def land(i, carry):
            slot[pl.ds(tab[0, i] - base, 1), :] = patch[pl.ds(i, 1), :]
            return carry

        lax.fori_loop(tab[2, j], tab[2, j + 1], land, 0)
        copies.append(pltpu.make_async_copy(slot, out_ref.at[at, :], sems.at[j % SLOTS]))
        copies[j].start()
    for copy in copies[-SLOTS:]:
        copy.wait()


def update(tile, held, incoming, returning, packed, tab):
    rows, cols = tile.shape
    vmem = pl.BlockSpec(memory_space=pltpu.VMEM)
    return pl.pallas_call(
        update_kernel,
        name="update",
        out_shape=jax.ShapeDtypeStruct((rows, cols), F32),
        in_specs=[pl.BlockSpec(memory_space=pltpu.SMEM)] + [vmem] * 5,
        out_specs=pl.BlockSpec(memory_space=pltpu.HBM),
        scratch_shapes=[
            pltpu.VMEM((SLOTS, TILE, cols), F32),
            pltpu.VMEM((3 * NB, cols), BF16),
            pltpu.VMEM((FEW, cols), F32),
            pltpu.SemaphoreType.DMA((SLOTS,)),
        ],
        compiler_params=pltpu.CompilerParams(vmem_limit_bytes=24 * 2**20),
    )(tab, tile, held, incoming, returning, packed)


def on_device(matrix, pivot_rows):
    tile, held, incoming, returning, packed, tab = exchange(matrix, pivot_rows)
    return update(tile, held, incoming, returning, packed, tab)


def solution(mesh):
    return jax.shard_map(
        on_device, mesh=mesh, in_specs=(P("prow", "pcol"), P()), out_specs=P("prow", "pcol"), check_vma=False
    )
```

time: 104 us -> 58.2 us (0.56)
  the two profiles are of different devices: /device:TPU:52 before, /device:TPU:8 now
where the time goes in v2:
time: 58.2 us
  Pallas kernels  57.5 us (99%)
  local copies, waits for them, and re-layouts  0.65 us (1%)
    pallas_call x1, Pallas kernels, exchange(): pl.pallas_call(exchange_kernel, name='exchange', out_shape=(jax.ShapeDtyp...  51.5 us
    pallas_call x1, Pallas kernels, update(): pl.pallas_call(update_kernel, name='update', out_shape=jax.ShapeDtypeStru...  6.03 us

profile of v2, /device:TPU:8, one launch (start us, length us, event | category | flops | bytes accessed | tf_op | source)
XLA Modules:
  0.0 58.2 jit_solution(10832640374175962188)
XLA Ops:
  0.0 0.0 copy-start
  0.0 0.7 %copy-done = s32[128]{0:T(128)S(1)} copy-done((s32[128]{0:T(128)S(1)}, s32[128]{0:T(128)}, u32[]{:S(2)}) %copy-start) | copy-done | bytes 536
  0.7 51.5 %exchange.1 = (f32[4096,384]{1,0:T(8,128)S(1)}, f32[4488,128]{1,0:T(8,128)S(1)}, f32[128,384]{1,0:T(8,128)S(1)}, f32[96,384]{1,0:T(8,128)S(1)}, f32[128,128]{1,0:T(8,128)S(1)}, /*index=5*/s32[8,128]{1,0:T(8,128)S(1)}) custom-call(s32[128]{0:T(128)S(1)} %copy-done, s32[1,128]{1,0:T(1,128)S(1)} %bitcast.1, f32[4096,384]{1,0:T(8,128)} %matrix.1), custom_call_target="tpu_custom_call" | custom-call | tf_op jit(solution)/shard_map/exchange/pallas_call | solution.py:437
  52.1 6.0 %update.1 = f32[4096,384]{1,0:T(8,128)} custom-call(s32[8,128]{1,0:T(8,128)S(1)} %get-tuple-element.11.tab, f32[4096,384]{1,0:T(8,128)S(1)} %get-tuple-element.12.tile_ref, f32[4488,128]{1,0:T(8,128)S(1)} %get-tuple-element.13.held, f32[128,384]{1,0:T(8,128)S(1)} %get-tuple-element.14.incoming_ref, f32[96,384]{1,0:T(8,128)S(1)} %get-tuple-element.15.returning_ref, ...), custom_call_target="tpu_custom_call" | custom-call | tf_op jit(solution)/shard_map/update/pallas_call | solution.py:539
Async XLA Ops:
  0.0 0.7 %copy-start = (s32[128]{0:T(128)S(1)}, s32[128]{0:T(128)}, u32[]{:S(2)}) copy-start(s32[128]{0:T(128)} %pivots_sm.1) | copy-start | bytes 1540

commit v3 on v2

v3 whole, which is shorter than its diff:
```python
import functools

import jax
import jax.numpy as jnp
from jax import lax
from jax.experimental import pallas as pl
from jax.experimental.pallas import tpu as pltpu
from jax.sharding import PartitionSpec as P

NB = 128
FEW = 96
F32 = jnp.float32
BF16 = jnp.bfloat16
I32 = jnp.int32
HIGH = lax.Precision.HIGHEST
MESH = pl.DeviceIdType.MESH

HOPS = (
    (1, 0, 0), (3, 0, 0), (2, 0, 0), (0, 1, 0), (0, 3, 0), (0, 2, 0),
    (0, 0, 1), (0, 0, 7), (0, 0, 2), (0, 0, 6), (0, 0, 3), (0, 0, 5), (0, 0, 4),
)
FAN = 4
PANEL_TREES = (
    (
        0, 0, 1537, 0, 6367233, 18480, 2060, 14352, 234930336, 624,
        112, 515, 0, 4, 0, 14337, 0, 0, 0, 0,
        12, 196996, 1540, 2052, 4, 515, 0, 4, 0, 0,
        0, 3, 0, 0, 0, 112, 0, 196993, 12, 12,
        513, 1, 513, 0, 3, 0, 0, 16, 112, 1539,
        0, 0, 4, 235078145, 1537, 12, 3, 2049, 4, 0,
        0, 14339, 0, 0, 196993, 12, 0, 0, 79884, 0,
        3, 4, 16, 0, 0, 515, 0, 0, 0, 0,
        0, 0, 112, 262284, 18612609, 25428481, 1837068, 235144708, 0, 262657,
        16, 16, 2050, 0, 14352, 16, 0, 0, 0, 0,
        12, 12, 12, 1, 0, 0, 0, 1, 0, 0,
        0, 0, 0, 0, 12, 0, 12, 12, 1539, 196739,
        515, 4, 0, 0, 0, 112, 0, 0,
    ),
    (
        0, 0, 0, 0, 0, 4, 131, 0, 12, 0,
        12, 0, 34091010, 0, 235089952, 0, 1, 1, 0, 0,
        3, 0, 0, 0, 0, 0, 1539, 14337, 132, 112,
        0, 234946956, 388, 16, 262659, 0, 63489, 112, 0, 0,
        400, 0, 63504, 0, 2294275, 0, 34080260, 112, 0, 0,
        0, 0, 3, 0, 0, 0, 197121, 1540, 12, 0,
        4, 0, 1, 0, 0, 3, 0, 14352, 385, 0,
        0, 0, 263683, 0, 0, 112, 196993, 263684, 197128, 4,
        0, 0, 515, 0, 385, 0, 0, 0, 0, 0,
        385, 0, 4, 0, 17924, 0, 515, 0, 3, 515,
        1837057, 2049, 0, 16, 400, 4, 2051, 0, 235078240, 0,
        30732, 0, 0, 16, 2049, 16, 12, 0, 0, 0,
        528, 0, 1537, 0, 0, 1540, 16899, 0,
    ),
    (
        0, 4, 0, 0, 3, 0, 0, 1648, 0, 0,
        0, 0, 63584, 0, 4, 0, 6488608, 0, 3, 12,
        240, 1, 14352, 0, 3, 1, 16, 12, 1537, 235144705,
        14340, 16, 0, 1, 0, 1, 0, 0, 0, 1,
        0, 12, 0, 0, 0, 17924, 0, 2060, 17411, 197121,
        16, 14340, 0, 528, 0, 63520, 235079683, 0, 16, 3,
        112, 144, 0, 0, 0, 0, 1, 0, 0, 513,
        0, 0, 1539, 0, 0, 12, 112, 4, 0, 3,
        112, 1, 0, 0, 0, 0, 0, 385, 0, 12,
        0, 1, 79875, 197121, 12, 624, 0, 1, 4, 0,
        0, 0, 0, 1, 0, 196993, 0, 1837068, 10224001, 30724,
        0, 67596, 1, 144, 0, 0, 0, 0, 0, 1,
        2049, 263792, 2060, 16, 197121, 1, 12, 4,
    ),
    (
        0, 3933700, 0, 79904, 4, 14416, 0, 132, 0, 0,
        3, 624, 0, 14337, 1552, 0, 0, 3, 0, 4,
        0, 0, 14339, 131, 0, 0, 0, 385, 0, 12,
        8651137, 1, 1537, 262768, 0, 235143681, 0, 0, 0, 18436,
        0, 0, 0, 240, 1, 2060, 12, 0, 12, 0,
        1836548, 33751425, 0, 0, 14339, 2052, 0, 0, 0, 2049,
        16, 0, 2060, 14352, 0, 1, 0, 0, 14348, 1539,
        0, 3, 0, 1835523, 0, 0, 0, 0, 0, 16,
        0, 0, 1, 0, 1540, 234946945, 2360836, 0, 16, 276484,
        235143681, 0, 0, 515, 0, 0, 12, 515, 0, 12,
        0, 3, 1, 0, 0, 0, 0, 0, 0, 0,
        262659, 1539, 524, 14339, 4, 14339, 0, 0, 4, 0,
        0, 0, 3, 1540, 2060, 0, 0, 0,
    ),
    (
        0, 0, 0, 0, 0, 1539, 0, 0, 0, 3,
        2052, 0, 0, 12, 0, 0, 0, 0, 112, 0,
        1, 16, 0, 14348, 0, 0, 0, 0, 14339, 4,
        0, 14348, 112, 396, 112, 0, 624, 0, 112, 79875,
        112, 14337, 0, 0, 112, 14337, 14337, 0, 25231745, 1837057,
        112, 14352, 1835393, 1, 16, 2160, 0, 8128513, 513, 0,
        14337, 12, 0, 0, 0, 2060, 16, 1539, 0, 0,
        16, 2049, 0, 263683, 0, 2051, 0, 2049, 16, 235143308,
        112, 515, 1, 0, 0, 0, 0, 0, 12, 0,
        0, 0, 0, 3, 0, 0, 49284, 196740, 0, 0,
        388, 513, 0, 0, 14340, 0, 14340, 4, 16, 0,
        0, 0, 1835139, 65676, 1540, 262664, 4, 2051, 16, 0,
        0, 0, 63504, 33634307, 0, 16, 0, 0,
    ),
    (
        0, 0, 79904, 235929992, 0, 12, 131, 0, 12, 4,
        3, 2158608, 0, 1, 0, 0, 0, 515, 1, 0,
        0, 0, 0, 0, 33751172, 0, 12, 49312, 112, 0,
        385, 0, 0, 112, 235078147, 0, 0, 2051, 33620353, 112,
        0, 0, 385, 0, 0, 2051, 1835393, 4, 112, 0,
        0, 0, 0, 0, 1, 0, 2049, 0, 0, 513,
        0, 0, 0, 513, 210960, 14340, 235078024, 65667, 14352, 0,
        0, 1, 0, 0, 235144707, 0, 0, 0, 235143553, 0,
        2051, 12, 515, 0, 0, 0, 385, 0, 0, 0,
        0, 14340, 0, 0, 0, 1, 0, 0, 3, 12,
        0, 0, 0, 12, 235078145, 235144708, 263684, 8128001, 0, 0,
        0, 0, 0, 3, 10224096, 1540, 1, 0, 0, 1,
        0, 0, 0, 1, 0, 0, 3, 33572355,
    ),
)
TAIL_TREES = (
    (
        0, 0, 2363404, 0, 1837104, 0, 0, 0, 1839106, 0,
        25223264, 0, 0, 0, 6322224, 0, 0, 112, 196993, 1,
        16899, 0, 0, 112, 513, 0, 0, 0, 0, 0,
        33751425, 0, 0, 0, 6308384, 0, 12, 0, 112, 0,
        8437920, 33751553, 0, 235144708, 16, 0, 0, 0, 0, 0,
        0, 0, 27001217, 1537, 0, 2060, 0, 0, 0, 0,
        0, 0, 25231745, 0, 0, 0, 515, 12, 1537, 0,
        0, 0, 1835393, 0, 0, 0, 1, 0, 0, 0,
        33620364, 0, 0, 235144708, 1835521, 263684, 0, 515, 16, 0,
        0, 0, 1837058, 0, 235078147, 16, 513, 1, 0, 2052,
        0, 0, 0, 0, 0, 0, 197121, 0, 1, 0,
        0, 0, 0, 0, 0, 0, 1, 263681, 0, 0,
        65921, 14340, 0, 2060, 2052, 0, 197121, 0,
    ),
    (
        0, 0, 0, 206896, 1839105, 25231536, 12, 0, 0, 0,
        0, 12, 0, 0, 0, 1836576, 25231490, 12, 1544, 0,
        3, 0, 0, 263684, 112, 0, 235144707, 0, 14348, 1837088,
        112, 0, 0, 0, 0, 1, 513, 235078145, 0, 0,
        0, 0, 0, 0, 0, 0, 0, 235078017, 0, 0,
        235078147, 235143560, 0, 2052, 0, 0, 0, 0, 0, 25231745,
        0, 0, 0, 0, 234948097, 263688, 0, 1539, 14340, 0,
        0, 0, 0, 0, 0, 0, 14338, 0, 0, 0,
        0, 0, 0, 6308360, 0, 0, 0, 14339, 197121, 0,
        0, 1835523, 0, 0, 0, 0, 3670280, 263684, 33751172, 2060,
        0, 14352, 33583106, 0, 1837058, 0, 33603808, 0, 0, 1837059,
        112, 0, 0, 0, 0, 0, 1539, 0, 0, 4,
        513, 0, 0, 0, 0, 0, 0, 3,
    ),
    (
        0, 1544, 0, 235149316, 0, 3, 4, 234946976, 0, 235144752,
        0, 1, 4098, 112, 2144, 0, 0, 0, 1835523, 197123,
        0, 0, 0, 1, 0, 196993, 0, 0, 0, 0,
        0, 1537, 14340, 0, 0, 0, 0, 0, 0, 25231746,
        0, 0, 0, 0, 25231490, 1836548, 197121, 0, 0, 0,
        0, 17924, 0, 0, 0, 385, 0, 25231745, 0, 0,
        0, 0, 0, 33751425, 0, 1836547, 1835144, 0, 0, 0,
        0, 0, 4, 0, 0, 0, 0, 0, 0, 0,
        8406018, 276492, 197232, 0, 235143553, 112, 14352, 1837068, 235143553, 1837057,
        0, 14352, 0, 2051, 14337, 0, 0, 0, 0, 1,
        1, 0, 0, 0, 4, 0, 0, 0, 0, 0,
        197121, 0, 1, 0, 0, 8128001, 0, 0, 0, 385,
        0, 196993, 0, 0, 0, 1, 0, 263681,
    ),
)
TURNS = (
    (
        0, 111616, 11, 98304, 270339, 11698629, 360, 175109, 453, 13631496,
        15040811, 262152, 3168, 11698187, 275648, 11, 3328, 459104, 15741952, 300032,
        12588491, 15736840, 470027, 16089096, 8205, 11275, 13792, 470475, 12588192, 16163072,
        371712, 16163181, 12878112, 9811424, 12583296, 207885, 9437536, 460, 15728655, 12892171,
        12583209, 15741963, 398, 360448, 9797835, 13052928, 16154912, 11566, 4560911, 7349260,
        9808896, 7644160, 7340492, 9448457, 13041676, 9808911, 9583, 12583372, 15744495, 471040,
        7813568, 9448463, 459136, 360448, 12, 9929199, 12597248, 9437664, 492009, 407552,
        15728655, 13041676, 12684, 16220160, 0, 15744495, 11552, 12597632, 15729056, 13056384,
        15739904, 12597248, 16220655, 12, 393671, 294921, 393228, 15369, 14123008, 407564,
        492015, 14348, 9514, 16231424, 14733, 11279, 5603616, 8662016, 14784, 262496,
        8388975, 11895244, 491535, 14796, 11534624, 13792, 14680448, 11545615, 13637824, 9216,
        426272, 369664, 3416064, 5418432, 8651117, 5407168, 11534795, 8388621, 11894795, 13320,
        8552, 11275, 11974112, 9811968, 365568, 8397165, 11552, 11264,
    ),
    (
        0, 458752, 453, 473091, 14784, 671755, 642056, 524288, 457, 557067,
        585, 642054, 458752, 524302, 557600, 16384, 14336, 17038, 640555, 524928,
        16896, 0, 0, 642656, 20075, 655360, 20491, 9, 16398, 19456,
        21134, 622592, 655360, 11, 585, 20480, 18048, 20494, 651, 655374,
        576, 640, 14, 640, 557696, 655374, 655371, 20494, 13, 0,
        20480, 608256, 576, 21120, 14, 656000, 15, 688128, 0, 21516,
        0, 0, 672, 655375, 18442, 675853, 688810, 21127, 21133, 0,
        0, 10, 688800, 0, 13, 0, 21120, 0, 13, 0,
        492013, 589838, 589835, 19008, 590400, 656000, 688142, 676480, 610944, 688128,
        0, 709644, 576, 655360, 688800, 655, 14912, 18048, 18443, 643727,
        655360, 20480, 20480, 12, 706572, 15, 22188, 9, 640, 20480,
        675840, 0, 622592, 11, 8, 524293, 16907, 608, 0, 642056,
        21024, 656000, 0, 651, 640, 622592, 651, 642056,
    ),
)
PANEL_ROOT = ((4,), (12,), (16, 12), (1, 3), (48, 112), (3,))
TAIL_ROOT = ((2, 8, 80, 4), (96, 3, 4, 16), (80, 1, 3, 12))
SPREAD = 15
TAIL_SPREAD = 21

TREES = len(PANEL_TREES)
TAILS = len(TAIL_TREES)
PIECE = 64
PANEL = 4096
CHUNKS = tuple(PANEL // PIECE // TREES + (t < PANEL // PIECE % TREES) for t in range(TREES))
MOST = CHUNKS[0]
FIRST = tuple(sum(CHUNKS[:t]) * PIECE for t in range(TREES))
INV = PANEL
TAIL = -(-2 * NB // (8 * TAILS)) * 8
HELD = INV + TAILS * TAIL
SOON = 2
EARLY = 4
TILE = 512


def swap_lists(pivot_col, pivot_row, row_start, tab_ref):
    lane = lax.broadcasted_iota(I32, (NB, NB), 1)
    sub = lax.broadcasted_iota(I32, (NB, NB), 0)
    low = pivot_col >= NB
    smaller = (pivot_row < pivot_col) & (pivot_row >= NB)
    rank = jnp.sum(jnp.where(smaller, 1.0, 0.0), axis=1, keepdims=True)
    lane_f = lane.astype(F32)
    hit = (rank == lane_f) & low
    landing = jnp.sum(jnp.where(hit, pivot_col.astype(F32), 0.0), axis=0, keepdims=True)
    chosen = jnp.sum(jnp.where(pivot_col == lane, 1.0, 0.0), axis=0, keepdims=True)
    free = jnp.broadcast_to(1.0 - chosen, (NB, NB))
    ahead = jnp.sum(jnp.where(lane < sub, free, 0.0), axis=1, keepdims=True)
    own = jnp.sum(jnp.where(lane == sub, free, 0.0), axis=1, keepdims=True)
    place = (ahead == lane_f) & (own > 0.5)
    displaced = jnp.sum(jnp.where(place, sub.astype(F32), 0.0), axis=0, keepdims=True)
    bound = row_start + lane * TILE
    starts = jnp.sum(jnp.where(low & (pivot_col < bound), 1.0, 0.0), axis=0, keepdims=True)
    tab_ref[...] = jnp.concatenate(
        [landing, displaced, starts, jnp.zeros((5, NB), F32)], axis=0
    ).astype(I32)


def pick(values, bits):
    while len(values) > 1:
        bit, bits = bits[0], bits[1:]
        values = [
            lo if isinstance(lo, int) and isinstance(hi, int) and lo == hi else jnp.where(bit, hi, lo)
            for lo, hi in zip(values[::2], values[1::2])
        ]
    return values[0]


def eliminate(
    block, packed_ref, linv_ref, binv_ref, upper_ref, scale_ref, busy_turns, busy, between
):
    lane = lax.broadcasted_iota(I32, (8, NB), 1)
    sub = lax.broadcasted_iota(I32, (8, NB), 0)
    groups = NB // 8
    rows = tuple(block[8 * q : 8 * q + 8, :] for q in range(groups))
    lower = tuple(jnp.zeros((8, NB), F32) for q in range(groups))

    def row_of(x, k):
        return jnp.broadcast_to(x[k : k + 1, :], (8, NB))

    def column_of(x, k):
        return jnp.broadcast_to(x[:, k : k + 1], (8, NB))

    def turn(g, carry, also=None):
        if also is not None:
            also(g)
        a, low = list(carry[0]), list(carry[1])
        seen, scale = a[0], jnp.zeros((8, NB), F32)
        column = [column_of(a[0], j) for j in range(8)]
        for k in range(8):
            pivot = row_of(column[k], k)
            row = row_of(a[0], k)
            inverse = 1.0 / pivot
            here = sub == k
            seen = jnp.where(here, row, seen)
            scale = jnp.where(here, inverse, scale)
            row = jnp.where(lane == k, pivot + 1.0, row)
            first = jnp.where(here, 0.0, column[k] * inverse)
            for j in range(k + 1, 8):
                column[j] = column[j] - first * row_of(column[j], k)
            kept = lane == 8 * g + k
            for q in range(groups):
                factor = first if q == 0 else column_of(a[q], k) * inverse
                a[q] = a[q] - factor * row
                low[q] = jnp.where(kept, factor, low[q])
            a[0] = jnp.where(here & (lane == k), 1.0, a[0])
        at = pl.ds(pl.multiple_of(8 * g, 8), 8)
        upper_ref[at, :] = seen
        scale_ref[at, :] = scale
        a = [pltpu.roll(x, NB - 8, 1) for x in a]
        return tuple(a[1:] + a[:1]), tuple(low[1:] + low[:1])

    carry = lax.fori_loop(0, busy_turns, functools.partial(turn, also=busy), (rows, lower))
    between()
    rows, lower = lax.fori_loop(busy_turns, groups, turn, carry)
    for q in range(groups):
        at = slice(8 * q, 8 * q + 8)
        seen = upper_ref[at, :]
        if q:
            seen = pltpu.roll(seen, 8 * q, 1)
        below = lane < sub + 8 * q
        packed_ref[at, :] = jnp.where(below, lower[q], seen)
        linv_ref[at, :] = jnp.where(below, seen, jnp.where(lane == sub + 8 * q, 1.0, 0.0))
        binv_ref[at, :] = rows[q] * scale_ref[at, :]


def exchange_kernel(
    pivots, matrix, tile_ref, held, incoming_ref, returning_ref, packed_ref, tab_ref,
    rows_ref, other, linv_ref, upper_ref, scale_ref, pivots_v, pivots_sm, tab_sm,
    arrive, depart, tail_arrive, tail_depart, root_depart, swap_sems, local_sems,
):
    plane, chip = lax.axis_index("prow"), lax.axis_index("pcol")
    rows_dev, cols = matrix.shape
    row_start = plane * rows_dev
    root = chip == 0

    fetch_sm = pltpu.make_async_copy(pivots, pivots_sm, local_sems.at[2])
    fetch_v = pltpu.make_async_copy(pivots, pivots_v, local_sems.at[3])
    fetch_v.start()
    fetch_sm.start()

    @pl.when(root)
    def _():
        for c in range(MOST):
            for t in range(TREES):
                if c < CHUNKS[t]:
                    lo = FIRST[t] + c * PIECE
                    pltpu.make_async_copy(
                        matrix.at[pl.ds(lo, PIECE), pl.ds(0, NB)],
                        held.at[pl.ds(lo, PIECE), :],
                        arrive.at[t, c],
                    ).start()
    load = pltpu.make_async_copy(matrix, tile_ref, local_sems.at[0])
    load.start()

    x, y, z = chip % 4, (chip // 4) % 4, chip // 16
    barrier = pltpu.get_barrier_semaphore()
    for dx, dy, dz in HOPS:
        there = (x + dx) % 4 + 4 * ((y + dy) % 4) + 16 * ((z + dz) % 8)
        pl.semaphore_signal(barrier, inc=1, device_id=(plane, there), device_id_type=MESH)
    pl.semaphore_signal(barrier, inc=1, device_id=(1 - plane, chip), device_id_type=MESH)

    fetch_v.wait()
    pivot_row = jnp.broadcast_to(pivots_v[...], (NB, NB))
    pivot_col = jnp.transpose(pivot_row.astype(F32)).astype(I32)
    swap_lists(pivot_col, pivot_row, row_start, tab_ref)
    move = pltpu.make_async_copy(tab_ref, tab_sm, local_sems.at[1])
    move.start()
    mine = (pivot_col >= row_start) & (pivot_col < row_start + rows_dev)

    def gather_pivots():
        fetch_sm.wait()
        load.wait()

        def some(i, carry):
            for j in range(8):
                k = 8 * i + j
                local = jnp.clip(pivots_sm[0, k] - row_start, 0, rows_dev - 1)
                rows_ref[pl.ds(k, 1), :] = tile_ref[pl.ds(local, 1), :]
            return carry

        lax.fori_loop(0, NB // 8, some, 0)
        swaps[0].start()
        swaps[1].start()

    def swap_of(i, rows, columns):
        return pltpu.make_async_remote_copy(
            src_ref=rows_ref.at[rows, columns], dst_ref=other.at[rows, columns],
            send_sem=swap_sems.at[i, 0], recv_sem=swap_sems.at[i, 1],
            device_id=(1 - plane, chip), device_id_type=MESH,
        )

    swaps = [
        swap_of(0, pl.ds(0, NB), pl.ds(0, NB)),
        swap_of(1, pl.ds(0, NB), pl.ds(NB, cols - NB)),
        swap_of(2, pl.ds(NB, FEW), pl.ds(0, cols)),
    ]

    def gather_displaced():
        move.wait()

        def some(i, carry):
            for j in range(8):
                k = 8 * i + j
                local = jnp.clip(tab_sm[1, k], 0, NB - 1)
                rows_ref[pl.ds(NB + k, 1), :] = tile_ref[pl.ds(local, 1), :]
            return carry

        lax.fori_loop(0, FEW // 8, some, 0)
        swaps[2].start()

    def merge(at):
        incoming_ref[:, at] = jnp.where(mine, rows_ref[:NB, at], other[:NB, at])

    def merge_rest():
        for j in range(1, cols // NB):
            merge(slice(j * NB, (j + 1) * NB))
        returning_ref[...] = jnp.where(plane == 0, rows_ref[NB:, :], other[NB:, :])

    def arrived(at, sem):
        pltpu.make_async_copy(held.at[at, :], held.at[at, :], sem).wait()

    def send(at, out_sem, in_sem, there):
        pltpu.make_async_remote_copy(
            src_ref=held.at[at, :], dst_ref=held.at[at, :], send_sem=out_sem, recv_sem=in_sem,
            device_id=(plane, there), device_id_type=MESH,
        ).start()

    def piece(t, c):
        return pl.ds(pl.multiple_of(FIRST[t] + c * PIECE, 8), PIECE)

    def tail(t):
        return pl.ds(INV + t * TAIL, TAIL)

    def offset(code):
        dx, dy, dz = code % 4, (code // 4) % 4, code // 16
        mirror = (4 - dx) % 4 + 4 * ((4 - dy) % 4) + 16 * ((8 - dz) % 8)
        return jnp.where(plane == 0, code, mirror)

    def steps(word):
        return [(word // 128**i) % 128 for i in range(FAN)]

    @pl.when(root)
    def _():
        def spread(c, trees=range(TREES)):
            for t in trees:
                at = piece(t, c)
                for i, code in enumerate(PANEL_ROOT[t]):
                    send(at, root_depart.at[t, i], arrive.at[t, c], offset(code))

        def staged(c):
            for t in range(TREES):
                if c < CHUNKS[t]:
                    arrived(piece(t, c), arrive.at[t, c])

        pl.semaphore_wait(barrier, len(HOPS) + 1)
        for c in range(SOON):
            staged(c)
            spread(c)
        gather_pivots()
        gather_displaced()
        for c in range(SOON, MOST):
            staged(c)
        for c in range(SOON, EARLY):
            spread(c)
        swaps[0].wait()
        merge(slice(0, NB))
        eliminate(
            incoming_ref[:, :NB], packed_ref, linv_ref, held.at[INV + NB : INV + 2 * NB, :],
            upper_ref, scale_ref, CHUNKS[-1] - EARLY, lambda g: spread(g + EARLY),
            lambda: spread(MOST - 1, [t for t in range(TREES) if CHUNKS[t] == MOST]),
        )
        swaps[1].wait()
        swaps[2].wait()
        held[INV : INV + NB, :] = linv_ref[...]

        @pl.when(plane == 1)
        def _():
            held[INV : INV + FEW, :] = other[NB:, :NB]

        if HELD > INV + 2 * NB:
            held[INV + 2 * NB : HELD, :] = jnp.zeros((HELD - INV - 2 * NB, NB), F32)
        for t in range(TAILS):
            for i, code in enumerate(TAIL_ROOT[t]):
                send(tail(t), root_depart.at[TREES + t, i], tail_arrive.at[t], offset(code))
        merge_rest()
        for t in range(TREES + TAILS):
            for i in range(len((PANEL_ROOT + TAIL_ROOT)[t])):
                at = pl.ds(0, CHUNKS[t] * PIECE if t < TREES else TAIL)
                arrived(at, root_depart.at[t, i])

    @pl.when(chip != 0)
    def _():
        place = jnp.where(plane == 0, chip, (4 - x) % 4 + 4 * ((4 - y) % 4) + 16 * ((8 - z) % 8))
        bits = [(place // (2**i)) % 2 == 1 for i in range(7)]

        def chips_of(word):
            codes, there = steps(word), []
            for code in codes:
                dx, dy, dz = code % 4, (code // 4) % 4, code // 16
                sign = 1 - 2 * plane
                there.append(
                    (x + sign * dx + 4) % 4 + 4 * ((y + sign * dy + 4) % 4)
                    + 16 * ((z + sign * dz + 8) % 8)
                )
            return codes, there

        panel = [chips_of(pick(list(table), bits)) for table in PANEL_TREES]
        turn_words = [pick(list(table), bits) for table in TURNS]
        turns = [(turn_words[t // 5] // 32 ** (t % 5)) % 32 for t in range(TREES + TAILS)]
        tails = [chips_of(pick(list(table), bits)) for table in TAIL_TREES]
        pl.semaphore_wait(barrier, len(HOPS) + 1)
        gather_pivots()
        gather_displaced()

        def send_all(node, at, out_sems, in_sem):
            codes, there = node
            send(at, out_sems.at[0], in_sem, there[0])

            @pl.when(codes[1] > 0)
            def _():
                send(at, out_sems.at[1], in_sem, there[1])

                @pl.when(codes[2] > 0)
                def _():
                    send(at, out_sems.at[2], in_sem, there[2])

                    @pl.when(codes[3] > 0)
                    def _():
                        send(at, out_sems.at[3], in_sem, there[3])

        def pass_on(s, carry):
            for t in range(TREES):
                c = s - turns[t]

                @pl.when((c >= 0) & (c < CHUNKS[t]) & (panel[t][0][0] > 0))
                def _():
                    at = piece(t, c)
                    arrived(at, arrive.at[t, c])
                    send_all(panel[t], at, depart.at[t], arrive.at[t, c])
            for t in range(TAILS):
                @pl.when((turns[TREES + t] == s) & (tails[t][0][0] > 0))
                def _():
                    arrived(tail(t), tail_arrive.at[t])
                    send_all(tails[t], tail(t), tail_depart.at[t], tail_arrive.at[t])
            return carry

        lax.fori_loop(1, max(SPREAD + MOST, TAIL_SPREAD + 1), pass_on, 0)
        for swap in swaps:
            swap.wait()
        merge(slice(0, NB))
        merge_rest()

        for t in range(TREES):
            @pl.when(panel[t][0][0] == 0)
            def _():
                for c in range(CHUNKS[t]):
                    arrived(piece(t, c), arrive.at[t, c])
        for t in range(TAILS):
            @pl.when(tails[t][0][0] == 0)
            def _():
                arrived(tail(t), tail_arrive.at[t])
        for t in range(TREES + TAILS):
            codes = (panel + tails)[t][0]
            for i in range(FAN):
                @pl.when(codes[i] > 0)
                def _():
                    if t < TREES:
                        arrived(pl.ds(0, CHUNKS[t] * PIECE), depart.at[t, i])
                    else:
                        arrived(pl.ds(0, TAIL), tail_depart.at[t - TREES, i])


def exchange(matrix, pivot_rows):
    rows, cols = matrix.shape
    vmem = pl.BlockSpec(memory_space=pltpu.VMEM)
    return pl.pallas_call(
        exchange_kernel,
        name="exchange",
        out_shape=(
            jax.ShapeDtypeStruct((rows, cols), F32),
            jax.ShapeDtypeStruct((HELD, NB), F32),
            jax.ShapeDtypeStruct((NB, cols), F32),
            jax.ShapeDtypeStruct((FEW, cols), F32),
            jax.ShapeDtypeStruct((NB, NB), F32),
            jax.ShapeDtypeStruct((8, NB), I32),
        ),
        in_specs=[pl.BlockSpec(memory_space=pltpu.HBM)] * 2,
        out_specs=(vmem,) * 6,
        scratch_shapes=[
            pltpu.VMEM((NB + FEW, cols), F32),
            pltpu.VMEM((NB + FEW, cols), F32),
            pltpu.VMEM((NB, NB), F32),
            pltpu.VMEM((NB, NB), F32),
            pltpu.VMEM((NB, NB), F32),
            pltpu.VMEM((1, NB), I32),
            pltpu.SMEM((1, NB), I32),
            pltpu.SMEM((8, NB), I32),
            pltpu.SemaphoreType.DMA((TREES, MOST)),
            pltpu.SemaphoreType.DMA((TREES, FAN)),
            pltpu.SemaphoreType.DMA((TAILS,)),
            pltpu.SemaphoreType.DMA((TAILS, FAN)),
            pltpu.SemaphoreType.DMA((TREES + TAILS, max(map(len, PANEL_ROOT + TAIL_ROOT)))),
            pltpu.SemaphoreType.DMA((3, 2)),
            pltpu.SemaphoreType.DMA((4,)),
        ],
        compiler_params=pltpu.CompilerParams(
            collective_id=0, has_side_effects=True, vmem_limit_bytes=44 * 2**20
        ),
    )(pivot_rows.reshape(1, NB), matrix)


SLOTS = 3


def update_kernel(
    tab, tile_ref, held, incoming_ref, returning_ref, packed_ref, out_ref,
    slots, right, patch, ext, sems,
):
    plane, first = lax.axis_index("prow"), lax.axis_index("pcol") == 0
    rows = tile_ref.shape[0]

    def product(left_f32):
        high = left_f32.astype(BF16)
        low = (left_f32 - high.astype(F32)).astype(BF16)
        return jnp.dot(
            jnp.concatenate([high, high, low], axis=1), right[...], preferred_element_type=F32
        )

    def keep(block):
        return jnp.concatenate([jnp.where(first, 0.0, block[:, :NB]), block[:, NB:]], axis=1)

    @pl.when(plane == 1)
    def _():
        ext[...] = held[INV : INV + FEW, :]

    @pl.when(plane == 0)
    def _():
        def take(i, carry):
            for k in range(8):
                row = jnp.clip(tab[1, 8 * i + k], 0, NB - 1)
                ext[pl.ds(8 * i + k, 1), :] = held[pl.ds(row, 1), :]
            return carry

        lax.fori_loop(0, FEW // 8, take, 0)

    source = incoming_ref[...]
    lane = lax.broadcasted_iota(I32, (NB, NB), 1)
    sub = lax.broadcasted_iota(I32, (NB, NB), 0)
    packed = packed_ref[...]
    unit = jnp.where(lane < sub, packed, jnp.where(lane == sub, 1.0, 0.0))
    w = jnp.dot(
        held[INV + NB : INV + 2 * NB, :],
        jnp.concatenate([jnp.where(first, -unit, source[:, :NB]), source[:, NB:]], axis=1),
        precision=HIGH, preferred_element_type=F32,
    )
    high = w.astype(BF16)
    right[0:NB, :] = high
    right[NB : 2 * NB, :] = (w - high.astype(F32)).astype(BF16)
    right[2 * NB :, :] = high
    patch[...] = keep(returning_ref[...]) - product(ext[...])

    copies = []
    for j in range(rows // TILE):
        slot = slots.at[j % SLOTS]
        if j >= SLOTS:
            copies[j - SLOTS].wait()
        at = slice(j * TILE, (j + 1) * TILE)
        slot[...] = keep(tile_ref[at, :]) - product(held[at, :])
        if j == 0:
            @pl.when(plane == 0)
            def _():
                upper = jnp.dot(
                    held[INV : INV + NB, :], source, precision=HIGH, preferred_element_type=F32
                )
                slot[0:NB, :] = jnp.concatenate(
                    [jnp.where(first, packed, upper[:, :NB]), upper[:, NB:]], axis=1
                )
        base = plane * rows + j * TILE

        def land(i, carry):
            slot[pl.ds(tab[0, i] - base, 1), :] = patch[pl.ds(i, 1), :]
            return carry

        lax.fori_loop(tab[2, j], tab[2, j + 1], land, 0)
        copies.append(pltpu.make_async_copy(slot, out_ref.at[at, :], sems.at[j % SLOTS]))
        copies[j].start()
    for copy in copies[-SLOTS:]:
        copy.wait()


def update(tile, held, incoming, returning, packed, tab):
    rows, cols = tile.shape
    vmem = pl.BlockSpec(memory_space=pltpu.VMEM)
    return pl.pallas_call(
        update_kernel,
        name="update",
        out_shape=jax.ShapeDtypeStruct((rows, cols), F32),
        in_specs=[pl.BlockSpec(memory_space=pltpu.SMEM)] + [vmem] * 5,
        out_specs=pl.BlockSpec(memory_space=pltpu.HBM),
        scratch_shapes=[
            pltpu.VMEM((SLOTS, TILE, cols), F32),
            pltpu.VMEM((3 * NB, cols), BF16),
            pltpu.VMEM((FEW, cols), F32),
            pltpu.VMEM((FEW, NB), F32),
            pltpu.SemaphoreType.DMA((SLOTS,)),
        ],
        compiler_params=pltpu.CompilerParams(vmem_limit_bytes=24 * 2**20),
    )(tab, tile, held, incoming, returning, packed)


def on_device(matrix, pivot_rows):
    tile, held, incoming, returning, packed, tab = exchange(matrix, pivot_rows)
    return update(tile, held, incoming, returning, packed, tab)


def solution(mesh):
    return jax.shard_map(
        on_device, mesh=mesh, in_specs=(P("prow", "pcol"), P()), out_specs=P("prow", "pcol"), check_vma=False
    )
```

time: 58.2 us -> 50.4 us (0.87)
  the two profiles are of different devices: /device:TPU:8 before, /device:TPU:2 now
where the time goes in v3:
time: 50.4 us; the launch traced here: 50.2 us
  Pallas kernels  49.6 us (98%)
  local copies, waits for them, and re-layouts  0.65 us (1%)
    pallas_call x1, Pallas kernels, exchange(): pl.pallas_call(exchange_kernel, name='exchange', out_shape=(jax.ShapeDtyp...  43.2 us
    pallas_call x1, Pallas kernels, update(): pl.pallas_call(update_kernel, name='update', out_shape=jax.ShapeDtypeStru...  6.36 us

profile of v3, /device:TPU:2, one launch (start us, length us, event | category | flops | bytes accessed | tf_op | source)
XLA Modules:
  0.0 50.2 jit_solution(7082693330159401550)
XLA Ops:
  0.0 0.0 copy-start
  0.0 0.7 %copy-done = s32[128]{0:T(128)S(1)} copy-done((s32[128]{0:T(128)S(1)}, s32[128]{0:T(128)}, u32[]{:S(2)}) %copy-start) | copy-done | bytes 536
  0.7 43.2 %exchange.1 = (f32[4096,384]{1,0:T(8,128)S(1)}, f32[4360,128]{1,0:T(8,128)S(1)}, f32[128,384]{1,0:T(8,128)S(1)}, f32[96,384]{1,0:T(8,128)S(1)}, f32[128,128]{1,0:T(8,128)S(1)}, /*index=5*/s32[8,128]{1,0:T(8,128)S(1)}) custom-call(s32[1,128]{1,0:T(1,128)S(1)} %bitcast.1, f32[4096,384]{1,0:T(8,128)} %matrix.1), custom_call_target="tpu_custom_call" | custom-call | tf_op jit(solution)/shard_map/exchange/pallas_call | solution.py:554
  43.9 6.4 %update.1 = f32[4096,384]{1,0:T(8,128)} custom-call(s32[8,128]{1,0:T(8,128)S(1)} %get-tuple-element.11.tab, f32[4096,384]{1,0:T(8,128)S(1)} %get-tuple-element.12.tile_ref, f32[4360,128]{1,0:T(8,128)S(1)} %get-tuple-element.13.held, f32[128,384]{1,0:T(8,128)S(1)} %get-tuple-element.14.incoming_ref, f32[96,384]{1,0:T(8,128)S(1)} %get-tuple-element.15.returning_ref, ...), custom_call_target="tpu_custom_call" | custom-call | tf_op jit(solution)/shard_map/update/pallas_call | solution.py:672
Async XLA Ops:
  0.0 0.7 %copy-start = (s32[128]{0:T(128)S(1)}, s32[128]{0:T(128)}, u32[]{:S(2)}) copy-start(s32[128]{0:T(128)} %param.3) | copy-start | bytes 1540

commit v4 on v3

--- a/solution.py
+++ b/solution.py
@@ -161,44 +161,44 @@
 )
 TURNS = (
     (
-        0, 111616, 11, 98304, 270339, 11698629, 360, 175109, 453, 13631496,
-        15040811, 262152, 3168, 11698187, 275648, 11, 3328, 459104, 15741952, 300032,
-        12588491, 15736840, 470027, 16089096, 8205, 11275, 13792, 470475, 12588192, 16163072,
-        371712, 16163181, 12878112, 9811424, 12583296, 207885, 9437536, 460, 15728655, 12892171,
-        12583209, 15741963, 398, 360448, 9797835, 13052928, 16154912, 11566, 4560911, 7349260,
-        9808896, 7644160, 7340492, 9448457, 13041676, 9808911, 9583, 12583372, 15744495, 471040,
-        7813568, 9448463, 459136, 360448, 12, 9929199, 12597248, 9437664, 492009, 407552,
-        15728655, 13041676, 12684, 16220160, 0, 15744495, 11552, 12597632, 15729056, 13056384,
-        15739904, 12597248, 16220655, 12, 393671, 294921, 393228, 15369, 14123008, 407564,
-        492015, 14348, 9514, 16231424, 14733, 11279, 5603616, 8662016, 14784, 262496,
-        8388975, 11895244, 491535, 14796, 11534624, 13792, 14680448, 11545615, 13637824, 9216,
-        426272, 369664, 3416064, 5418432, 8651117, 5407168, 11534795, 8388621, 11894795, 13320,
-        8552, 11275, 11974112, 9811968, 365568, 8397165, 11552, 11264,
-    ),
-    (
-        0, 458752, 453, 473091, 14784, 671755, 642056, 524288, 457, 557067,
-        585, 642054, 458752, 524302, 557600, 16384, 14336, 17038, 640555, 524928,
-        16896, 0, 0, 642656, 20075, 655360, 20491, 9, 16398, 19456,
-        21134, 622592, 655360, 11, 585, 20480, 18048, 20494, 651, 655374,
-        576, 640, 14, 640, 557696, 655374, 655371, 20494, 13, 0,
-        20480, 608256, 576, 21120, 14, 656000, 15, 688128, 0, 21516,
-        0, 0, 672, 655375, 18442, 675853, 688810, 21127, 21133, 0,
-        0, 10, 688800, 0, 13, 0, 21120, 0, 13, 0,
-        492013, 589838, 589835, 19008, 590400, 656000, 688142, 676480, 610944, 688128,
-        0, 709644, 576, 655360, 688800, 655, 14912, 18048, 18443, 643727,
-        655360, 20480, 20480, 12, 706572, 15, 22188, 9, 640, 20480,
-        675840, 0, 622592, 11, 8, 524293, 16907, 608, 0, 642056,
-        21024, 656000, 0, 651, 640, 622592, 651, 642056,
+        0, 1417216, 21, 1310720, 4259845, 355206923, 1424, 2969611, 1803, 436207632,
+        475268181, 4194320, 20800, 355205141, 4301568, 21, 21504, 7341376, 486645760, 4501504,
+        402700053, 486604816, 7426069, 492306448, 65562, 86037, 108352, 7427861, 402698944, 493421568,
+        5591040, 493421978, 407110720, 307865408, 402654720, 3235866, 301991296, 1816, 486539293, 407224341,
+        402654289, 486645782, 1564, 5767168, 307757846, 410079232, 493356160, 87132, 140034077, 218173464,
+        307847168, 222629888, 218105624, 302080018, 409993240, 307847197, 75165, 402655000, 486659933, 7438336,
+        225560320, 302080029, 7341568, 5767168, 24, 309593949, 402767872, 301991744, 7604050, 6406144,
+        486539293, 409993240, 99864, 494141440, 0, 486659933, 91264, 402769408, 486540864, 410109440,
+        486629376, 402767872, 494143325, 24, 6293261, 4718610, 6291480, 118802, 443809792, 6406168,
+        7604061, 114712, 70740, 494231552, 116250, 90141, 190055488, 272719872, 116480, 4195712,
+        268436893, 357828376, 7602205, 116504, 352322624, 108352, 469763584, 369188893, 436257536, 69632,
+        6816896, 5574656, 88145920, 187520768, 272631194, 187434752, 352323349, 268435482, 357826581, 106512,
+        66960, 86037, 376022848, 290832384, 5550080, 268502426, 87104, 90112,
+    ),
+    (
+        0, 7077888, 1867, 7188485, 112320, 10358805, 10117136, 8650752, 1873, 8912918,
+        2257, 10117132, 7077888, 8650780, 8915072, 135168, 110592, 137692, 10102934, 8653248,
+        137280, 0, 0, 10119552, 158102, 10223616, 163862, 17, 135196, 155648,
+        162268, 9961472, 10223616, 22, 2257, 163840, 141824, 159772, 2582, 10223644,
+        2240, 2560, 28, 2560, 8915456, 10223644, 10485782, 159772, 25, 0,
+        163840, 9318400, 2240, 166400, 28, 10488320, 29, 11010048, 0, 172056,
+        0, 0, 2688, 10485789, 143380, 10649625, 11012756, 166415, 166425, 0,
+        0, 20, 11012736, 0, 26, 0, 166400, 0, 25, 0,
+        7866265, 9175068, 9699350, 145600, 9177280, 10488320, 11010076, 10652160, 9865728, 11010048,
+        0, 11182104, 2240, 10485760, 11012736, 2589, 121024, 141824, 143381, 10127901,
+        10485760, 159744, 163840, 24, 11153432, 29, 174744, 18, 2560, 159744,
+        10649600, 0, 9961472, 21, 16, 8650763, 137301, 2432, 0, 10117136,
+        166016, 10226112, 0, 2517, 2496, 9961472, 2517, 10117136,
     ),
 )
 PANEL_ROOT = ((4,), (12,), (16, 12), (1, 3), (48, 112), (3,))
 TAIL_ROOT = ((2, 8, 80, 4), (96, 3, 4, 16), (80, 1, 3, 12))
-SPREAD = 15
-TAIL_SPREAD = 21
+SPREAD = 29
+TAIL_SPREAD = 42
 
 TREES = len(PANEL_TREES)
 TAILS = len(TAIL_TREES)
-PIECE = 64
+PIECE = 32
 PANEL = 4096
 CHUNKS = tuple(PANEL // PIECE // TREES + (t < PANEL // PIECE % TREES) for t in range(TREES))
 MOST = CHUNKS[0]
@@ -206,8 +206,8 @@
 INV = PANEL
 TAIL = -(-2 * NB // (8 * TAILS)) * 8
 HELD = INV + TAILS * TAIL
-SOON = 2
-EARLY = 4
+SOON = 4
+EARLY = 8
 TILE = 512
 
 
@@ -302,8 +302,8 @@
 
 
 def exchange_kernel(
-    pivots, matrix, tile_ref, held, incoming_ref, returning_ref, packed_ref, tab_ref,
-    rows_ref, other, linv_ref, upper_ref, scale_ref, pivots_v, pivots_sm, tab_sm,
+    pivots, matrix, tile_ref, held, returning_ref, right, top, tab_ref,
+    incoming_ref, packed_ref, rows_ref, other, linv_ref, upper_ref, scale_ref, pivots_v, pivots_sm, tab_sm,
     arrive, depart, tail_arrive, tail_depart, root_depart, swap_sems, local_sems,
 ):
     plane, chip = lax.axis_index("prow"), lax.axis_index("pcol")
@@ -393,6 +393,31 @@
         for j in range(1, cols // NB):
             merge(slice(j * NB, (j + 1) * NB))
         returning_ref[...] = jnp.where(plane == 0, rows_ref[NB:, :], other[NB:, :])
+
+    def prepare():
+        source = incoming_ref[...]
+        lane = lax.broadcasted_iota(I32, (NB, NB), 1)
+        sub = lax.broadcasted_iota(I32, (NB, NB), 0)
+        packed = packed_ref[...]
+        unit = jnp.where(lane < sub, packed, jnp.where(lane == sub, 1.0, 0.0))
+        w = jnp.dot(
+            held[INV + NB : INV + 2 * NB, :],
+            jnp.concatenate([jnp.where(root, -unit, source[:, :NB]), source[:, NB:]], axis=1),
+            precision=HIGH, preferred_element_type=F32,
+        )
+        high = w.astype(BF16)
+        right[0:NB, :] = high
+        right[NB : 2 * NB, :] = (w - high.astype(F32)).astype(BF16)
+        right[2 * NB :, :] = high
+
+        @pl.when(plane == 0)
+        def _():
+            upper = jnp.dot(
+                held[INV : INV + NB, :], source, precision=HIGH, preferred_element_type=F32
+            )
+            top[...] = jnp.concatenate(
+                [jnp.where(root, packed, upper[:, :NB]), upper[:, NB:]], axis=1
+            )
 
     def arrived(at, sem):
         pltpu.make_async_copy(held.at[at, :], held.at[at, :], sem).wait()
@@ -461,6 +486,7 @@
             for i, code in enumerate(TAIL_ROOT[t]):
                 send(tail(t), root_depart.at[TREES + t, i], tail_arrive.at[t], offset(code))
         merge_rest()
+        prepare()
         for t in range(TREES + TAILS):
             for i in range(len((PANEL_ROOT + TAIL_ROOT)[t])):
                 at = pl.ds(0, CHUNKS[t] * PIECE if t < TREES else TAIL)
@@ -484,7 +510,7 @@
 
         panel = [chips_of(pick(list(table), bits)) for table in PANEL_TREES]
         turn_words = [pick(list(table), bits) for table in TURNS]
-        turns = [(turn_words[t // 5] // 32 ** (t % 5)) % 32 for t in range(TREES + TAILS)]
+        turns = [(turn_words[t // 5] // 64 ** (t % 5)) % 64 for t in range(TREES + TAILS)]
         tails = [chips_of(pick(list(table), bits)) for table in TAIL_TREES]
         pl.semaphore_wait(barrier, len(HOPS) + 1)
         gather_pivots()
@@ -528,15 +554,16 @@
         merge(slice(0, NB))
         merge_rest()
 
+        for t in range(TAILS):
+            @pl.when(tails[t][0][0] == 0)
+            def _():
+                arrived(tail(t), tail_arrive.at[t])
+        prepare()
         for t in range(TREES):
             @pl.when(panel[t][0][0] == 0)
             def _():
                 for c in range(CHUNKS[t]):
                     arrived(piece(t, c), arrive.at[t, c])
-        for t in range(TAILS):
-            @pl.when(tails[t][0][0] == 0)
-            def _():
-                arrived(tail(t), tail_arrive.at[t])
         for t in range(TREES + TAILS):
             codes = (panel + tails)[t][0]
             for i in range(FAN):
@@ -557,14 +584,16 @@
         out_shape=(
             jax.ShapeDtypeStruct((rows, cols), F32),
             jax.ShapeDtypeStruct((HELD, NB), F32),
+            jax.ShapeDtypeStruct((FEW, cols), F32),
+            jax.ShapeDtypeStruct((3 * NB, cols), BF16),
             jax.ShapeDtypeStruct((NB, cols), F32),
-            jax.ShapeDtypeStruct((FEW, cols), F32),
-            jax.ShapeDtypeStruct((NB, NB), F32),
             jax.ShapeDtypeStruct((8, NB), I32),
         ),
         in_specs=[pl.BlockSpec(memory_space=pltpu.HBM)] * 2,
         out_specs=(vmem,) * 6,
         scratch_shapes=[
+            pltpu.VMEM((NB, cols), F32),
+            pltpu.VMEM((NB, NB), F32),
             pltpu.VMEM((NB + FEW, cols), F32),
             pltpu.VMEM((NB + FEW, cols), F32),
             pltpu.VMEM((NB, NB), F32),
@@ -591,8 +620,7 @@
 
 
 def update_kernel(
-    tab, tile_ref, held, incoming_ref, returning_ref, packed_ref, out_ref,
-    slots, right, patch, ext, sems,
+    tab, tile_ref, held, returning_ref, right, top, out_ref, slots, patch, ext, sems,
 ):
     plane, first = lax.axis_index("prow"), lax.axis_index("pcol") == 0
     rows = tile_ref.shape[0]
@@ -621,20 +649,6 @@
 
         lax.fori_loop(0, FEW // 8, take, 0)
 
-    source = incoming_ref[...]
-    lane = lax.broadcasted_iota(I32, (NB, NB), 1)
-    sub = lax.broadcasted_iota(I32, (NB, NB), 0)
-    packed = packed_ref[...]
-    unit = jnp.where(lane < sub, packed, jnp.where(lane == sub, 1.0, 0.0))
-    w = jnp.dot(
-        held[INV + NB : INV + 2 * NB, :],
-        jnp.concatenate([jnp.where(first, -unit, source[:, :NB]), source[:, NB:]], axis=1),
-        precision=HIGH, preferred_element_type=F32,
-    )
-    high = w.astype(BF16)
-    right[0:NB, :] = high
-    right[NB : 2 * NB, :] = (w - high.astype(F32)).astype(BF16)
-    right[2 * NB :, :] = high
     patch[...] = keep(returning_ref[...]) - product(ext[...])
 
     copies = []
@@ -647,12 +661,7 @@
         if j == 0:
             @pl.when(plane == 0)
             def _():
-                upper = jnp.dot(
-                    held[INV : INV + NB, :], source, precision=HIGH, preferred_element_type=F32
-                )
-                slot[0:NB, :] = jnp.concatenate(
-                    [jnp.where(first, packed, upper[:, :NB]), upper[:, NB:]], axis=1
-                )
+                slot[0:NB, :] = top[...]
         base = plane * rows + j * TILE
 
         def land(i, carry):
@@ -666,7 +675,7 @@
         copy.wait()
 
 
-def update(tile, held, incoming, returning, packed, tab):
+def update(tile, held, returning, right, top, tab):
     rows, cols = tile.shape
     vmem = pl.BlockSpec(memory_space=pltpu.VMEM)
     return pl.pallas_call(
@@ -677,18 +686,16 @@
         out_specs=pl.BlockSpec(memory_space=pltpu.HBM),
         scratch_shapes=[
             pltpu.VMEM((SLOTS, TILE, cols), F32),
-            pltpu.VMEM((3 * NB, cols), BF16),
             pltpu.VMEM((FEW, cols), F32),
             pltpu.VMEM((FEW, NB), F32),
             pltpu.SemaphoreType.DMA((SLOTS,)),
         ],
         compiler_params=pltpu.CompilerParams(vmem_limit_bytes=24 * 2**20),
-    )(tab, tile, held, incoming, returning, packed)
+    )(tab, tile, held, returning, right, top)
 
 
 def on_device(matrix, pivot_rows):
-    tile, held, incoming, returning, packed, tab = exchange(matrix, pivot_rows)
-    return update(tile, held, incoming, returning, packed, tab)
+    return update(*exchange(matrix, pivot_rows))
 
 
 def solution(mesh):

time: 50.4 us -> 48.6 us (0.964)
  Pallas kernels: 49.6 us -> 47.8 us
    pallas_call x1, Pallas kernels: 43.2 us -> 42 us  [exchange(): pl.pallas_call(exchange_kernel, name='exchange', out_shape=(jax.ShapeDtyp...]
    pallas_call x1, Pallas kernels: 6.36 us -> 5.76 us  [update(): pl.pallas_call(update_kernel, name='update', out_shape=jax.ShapeDtypeStru...]
where the time goes in v4:
time: 48.6 us; the launch traced here: 48.5 us
  Pallas kernels  47.8 us (98%)
  local copies, waits for them, and re-layouts  0.65 us (1%)
    pallas_call x1, Pallas kernels, exchange(): pl.pallas_call(exchange_kernel, name='exchange', out_shape=(jax.ShapeDtyp...  42 us
    pallas_call x1, Pallas kernels, update(): pl.pallas_call(update_kernel, name='update', out_shape=jax.ShapeDtypeStru...  5.76 us

profile of v4, /device:TPU:2, one launch (start us, length us, event | category | flops | bytes accessed | tf_op | source)
XLA Modules:
  0.0 48.5 jit_solution(18008311067037670628)
XLA Ops:
  0.0 0.0 copy-start
  0.0 0.7 %copy-done = s32[128]{0:T(128)S(1)} copy-done((s32[128]{0:T(128)S(1)}, s32[128]{0:T(128)}, u32[]{:S(2)}) %copy-start) | copy-done | bytes 536
  0.7 42.0 %exchange.1 = (f32[4096,384]{1,0:T(8,128)S(1)}, f32[4360,128]{1,0:T(8,128)S(1)}, f32[96,384]{1,0:T(8,128)S(1)}, bf16[384,384]{1,0:T(8,128)(2,1)S(1)}, f32[128,384]{1,0:T(8,128)S(1)}, /*index=5*/s32[8,128]{1,0:T(8,128)S(1)}) custom-call(s32[1,128]{1,0:T(1,128)S(1)} %bitcast.1, f32[4096,384]{1,0:T(8,128)} %matrix.1), custom_call_target="tpu_custom_call" | custom-call | tf_op jit(solution)/shard_map/exchange/pallas_call | solution.py:581
  42.7 5.8 %update.1 = f32[4096,384]{1,0:T(8,128)} custom-call(s32[8,128]{1,0:T(8,128)S(1)} %get-tuple-element.11.tab, f32[4096,384]{1,0:T(8,128)S(1)} %get-tuple-element.12.tile_ref, f32[4360,128]{1,0:T(8,128)S(1)} %get-tuple-element.13.held, f32[96,384]{1,0:T(8,128)S(1)} %get-tuple-element.14.returning_ref, bf16[384,384]{1,0:T(8,128)(2,1)S(1)} %get-tuple-element.15.right, ...), custom_call_target="tpu_custom_call" | custom-call | tf_op jit(solution)/shard_map/update/pallas_call | solution.py:681
Async XLA Ops:
  0.0 0.7 %copy-start = (s32[128]{0:T(128)S(1)}, s32[128]{0:T(128)}, u32[]{:S(2)}) copy-start(s32[128]{0:T(128)} %param.3) | copy-start | bytes 1540

commit v5 on v4

--- a/solution.py
+++ b/solution.py
@@ -161,40 +161,40 @@
 )
 TURNS = (
     (
-        0, 1417216, 21, 1310720, 4259845, 355206923, 1424, 2969611, 1803, 436207632,
-        475268181, 4194320, 20800, 355205141, 4301568, 21, 21504, 7341376, 486645760, 4501504,
-        402700053, 486604816, 7426069, 492306448, 65562, 86037, 108352, 7427861, 402698944, 493421568,
-        5591040, 493421978, 407110720, 307865408, 402654720, 3235866, 301991296, 1816, 486539293, 407224341,
-        402654289, 486645782, 1564, 5767168, 307757846, 410079232, 493356160, 87132, 140034077, 218173464,
-        307847168, 222629888, 218105624, 302080018, 409993240, 307847197, 75165, 402655000, 486659933, 7438336,
-        225560320, 302080029, 7341568, 5767168, 24, 309593949, 402767872, 301991744, 7604050, 6406144,
-        486539293, 409993240, 99864, 494141440, 0, 486659933, 91264, 402769408, 486540864, 410109440,
-        486629376, 402767872, 494143325, 24, 6293261, 4718610, 6291480, 118802, 443809792, 6406168,
-        7604061, 114712, 70740, 494231552, 116250, 90141, 190055488, 272719872, 116480, 4195712,
-        268436893, 357828376, 7602205, 116504, 352322624, 108352, 469763584, 369188893, 436257536, 69632,
-        6816896, 5574656, 88145920, 187520768, 272631194, 187434752, 352323349, 268435482, 357826581, 106512,
-        66960, 86037, 376022848, 290832384, 5550080, 268502426, 87104, 90112,
-    ),
-    (
-        0, 7077888, 1867, 7188485, 112320, 10358805, 10117136, 8650752, 1873, 8912918,
-        2257, 10117132, 7077888, 8650780, 8915072, 135168, 110592, 137692, 10102934, 8653248,
-        137280, 0, 0, 10119552, 158102, 10223616, 163862, 17, 135196, 155648,
-        162268, 9961472, 10223616, 22, 2257, 163840, 141824, 159772, 2582, 10223644,
-        2240, 2560, 28, 2560, 8915456, 10223644, 10485782, 159772, 25, 0,
-        163840, 9318400, 2240, 166400, 28, 10488320, 29, 11010048, 0, 172056,
-        0, 0, 2688, 10485789, 143380, 10649625, 11012756, 166415, 166425, 0,
-        0, 20, 11012736, 0, 26, 0, 166400, 0, 25, 0,
-        7866265, 9175068, 9699350, 145600, 9177280, 10488320, 11010076, 10652160, 9865728, 11010048,
-        0, 11182104, 2240, 10485760, 11012736, 2589, 121024, 141824, 143381, 10127901,
-        10485760, 159744, 163840, 24, 11153432, 29, 174744, 18, 2560, 159744,
-        10649600, 0, 9961472, 21, 16, 8650763, 137301, 2432, 0, 10117136,
-        166016, 10226112, 0, 2517, 2496, 9961472, 2517, 10117136,
+        0, 1970176, 26, 1835008, 5324807, 439617741, 1812, 3514381, 2253, 553648148,
+        594019674, 5242900, 29120, 439615514, 5379008, 26, 29952, 9176704, 604114944, 5558272,
+        503371994, 604061716, 9281562, 611319828, 81953, 106522, 137472, 9283802, 503370560, 612713728,
+        6922240, 612714273, 508822848, 393353472, 503318400, 4046881, 385877760, 2270, 603979812, 508964890,
+        503317845, 604114972, 1955, 7340032, 393216988, 512598016, 612632000, 107875, 175173668, 285298718,
+        393330688, 290803712, 285214942, 385990679, 512491550, 393330724, 96036, 503318750, 604129572, 9297920,
+        294533312, 385990692, 9176960, 7340032, 30, 395315492, 503459840, 385878272, 9439511, 8007680,
+        603979812, 512491550, 124830, 613416960, 0, 604129572, 116160, 503461760, 603981760, 512636800,
+        604094464, 503459840, 613419300, 30, 7866577, 6029335, 7864350, 147479, 563085312, 8007710,
+        9439524, 143390, 87385, 613531648, 145313, 114724, 224920896, 340901888, 145600, 5244672,
+        335546148, 443025630, 9437220, 145630, 436208960, 137472, 587204480, 469876772, 553710528, 86016,
+        8652224, 6901760, 122765312, 221620416, 340789025, 221513920, 436209882, 335544353, 443023386, 135188,
+        83732, 106522, 478550272, 359280640, 6868992, 335628065, 107840, 114688,
+    ),
+    (
+        0, 8912896, 2253, 9052167, 141440, 12746778, 12513300, 10485760, 2261, 11010076,
+        2837, 12513295, 8912896, 10485795, 11012736, 163840, 139264, 166947, 12495516, 10488832,
+        166400, 0, 0, 12516288, 195548, 12582912, 204828, 21, 163875, 192512,
+        199715, 12320768, 12582912, 28, 2837, 204800, 175232, 196643, 3228, 12582947,
+        2816, 3200, 35, 3200, 11013248, 12582947, 13107228, 196643, 31, 0,
+        204800, 11714560, 2816, 208000, 35, 13110400, 36, 13631488, 0, 213022,
+        0, 0, 3328, 13107236, 180249, 13312031, 13634841, 208018, 208031, 0,
+        0, 25, 13634816, 0, 33, 0, 208000, 0, 31, 0,
+        9701727, 11534371, 11796508, 183040, 11537152, 13110400, 13631523, 13315200, 12004480, 13631488,
+        0, 13844510, 2816, 13107200, 13634816, 3236, 146176, 175232, 180250, 12528804,
+        13107200, 196608, 204800, 30, 13811742, 36, 216350, 23, 3200, 196608,
+        13312000, 0, 12320768, 26, 20, 10485773, 166426, 3008, 0, 12513300,
+        207488, 12585984, 0, 3098, 3072, 12320768, 3098, 12513300,
     ),
 )
 PANEL_ROOT = ((4,), (12,), (16, 12), (1, 3), (48, 112), (3,))
 TAIL_ROOT = ((2, 8, 80, 4), (96, 3, 4, 16), (80, 1, 3, 12))
-SPREAD = 29
-TAIL_SPREAD = 42
+SPREAD = 36
+TAIL_SPREAD = 52
 
 TREES = len(PANEL_TREES)
 TAILS = len(TAIL_TREES)

time: 48.6 us -> 48.2 us (level)
  no operation moved by 1% of the time
where the time goes in v5:
time: 48.2 us; the launch traced here: 48.1 us
  Pallas kernels  47.4 us (98%)
  local copies, waits for them, and re-layouts  0.65 us (1%)
    pallas_call x1, Pallas kernels, exchange(): pl.pallas_call(exchange_kernel, name='exchange', out_shape=(jax.ShapeDtyp...  41.7 us
    pallas_call x1, Pallas kernels, update(): pl.pallas_call(update_kernel, name='update', out_shape=jax.ShapeDtypeStru...  5.73 us

profile of v5, /device:TPU:2, one launch (start us, length us, event | category | flops | bytes accessed | tf_op | source)
XLA Modules:
  0.0 48.1 jit_solution(3317766815269550754)
XLA Ops:
  0.0 0.0 copy-start
  0.0 0.7 %copy-done = s32[128]{0:T(128)S(1)} copy-done((s32[128]{0:T(128)S(1)}, s32[128]{0:T(128)}, u32[]{:S(2)}) %copy-start) | copy-done | bytes 536
  0.7 41.7 %exchange.1 = (f32[4096,384]{1,0:T(8,128)S(1)}, f32[4360,128]{1,0:T(8,128)S(1)}, f32[96,384]{1,0:T(8,128)S(1)}, bf16[384,384]{1,0:T(8,128)(2,1)S(1)}, f32[128,384]{1,0:T(8,128)S(1)}, /*index=5*/s32[8,128]{1,0:T(8,128)S(1)}) custom-call(s32[1,128]{1,0:T(1,128)S(1)} %bitcast.1, f32[4096,384]{1,0:T(8,128)} %matrix.1), custom_call_target="tpu_custom_call" | custom-call | tf_op jit(solution)/shard_map/exchange/pallas_call | solution.py:581
  42.4 5.7 %update.1 = f32[4096,384]{1,0:T(8,128)} custom-call(s32[8,128]{1,0:T(8,128)S(1)} %get-tuple-element.11.tab, f32[4096,384]{1,0:T(8,128)S(1)} %get-tuple-element.12.tile_ref, f32[4360,128]{1,0:T(8,128)S(1)} %get-tuple-element.13.held, f32[96,384]{1,0:T(8,128)S(1)} %get-tuple-element.14.returning_ref, bf16[384,384]{1,0:T(8,128)(2,1)S(1)} %get-tuple-element.15.right, ...), custom_call_target="tpu_custom_call" | custom-call | tf_op jit(solution)/shard_map/update/pallas_call | solution.py:681
Async XLA Ops:
  0.0 0.7 %copy-start = (s32[128]{0:T(128)S(1)}, s32[128]{0:T(128)}, u32[]{:S(2)}) copy-start(s32[128]{0:T(128)} %param.3) | copy-start | bytes 1540
